TPU v7x, 32 devices: a whole 2x2x4 slice. The times are simulated.
32 devices in a mesh: grp: 2 (over y), kz: 4 (over z), coil: 2 (over x), kx: 2 (over core).
Axes of the slice: x: 2, y: 2, z: 4, core: 2. Of those that a mesh axis runs over, the one named last changes fastest.
Arguments:
- measured: float32 [2, 64, 32, 32, 32], P(None, ('grp', 'coil'), 'kx', 'kz'), parts along dimension 1, may hold values from -6 to 6
- mask: int32 [64, 32, 32], P(('grp', 'kx'), 'kz'), parts along dimension 0, may hold values 0 or 1
- kernel: float32 [27, 2, 32, 64], P(None, None, 'coil'), may hold values from -0.109375 to 0.109375
Outputs:
- restored: float32 [2, 64, 32, 32, 32], P(None, ('grp', 'coil'), 'kx', 'kz'), parts along dimension 1
There are 2 independent parts, one for each index of `grp`. A program takes and returns all parts, laid end to end along the dimension named above; an argument that names none is the same for every part. Nothing has to cross between parts.
All inputs are finite; a program needn't handle non-finite values. No bound on the sum of `mask` on one device may be relied on, other than what follows from the above.
Results may differ from a plain program's by a relative error of at most 0.0001.
Values sent between devices are 32-bit elements; how exact they have to be, the bound alone decides.
A program may use at most 128 MiB of HBM per device.

v0:
```python
import functools

import jax
import jax.numpy as jnp
from jax import lax
from jax.experimental import pallas as pl
from jax.experimental.pallas import tpu as pltpu
from jax.sharding import PartitionSpec as P

ITERS = 2
LANES = 128
MESH = pl.DeviceIdType.MESH


def order(n, count, turn):
    odd = (n + turn) % 2
    return (1 - odd) * (count // 2 - 1 - n // 2) + odd * (count // 2 + n // 2)


def place_weights(kernel, shards, wf, target, low):
    taps, _, coils, inputs = kernel.shape
    width = 2 * inputs
    half = inputs // 2
    shape = (inputs, 2 * width)
    d = lax.broadcasted_iota(jnp.int32, shape, 0)
    q = lax.broadcasted_iota(jnp.int32, shape, 1)
    v, po = q // width, (q // inputs) % 2
    at = q % inputs
    pi, source = (at // coils) % 2, v * half + (at // (2 * coils)) * coils + at % coils
    hit = d == source
    real = jnp.where(hit & (po == pi), jnp.where((v == 1) & (po == 1), -1.0, 1.0), 0.0).astype(jnp.bfloat16)
    imag = jnp.where(hit & (po != pi), jnp.where((v == 0) & (po == 0), -1.0, 1.0), 0.0).astype(jnp.bfloat16)
    picked = (jnp.dot(split(kernel[:, 0].reshape(taps * coils, inputs))[low], real, preferred_element_type=jnp.float32)
              + jnp.dot(split(kernel[:, 1].reshape(taps * coils, inputs))[low], imag, preferred_element_type=jnp.float32))
    for v in range(2):
        for b in range(3):
            for a in range(3):
                for po in range(2):
                    parts = []
                    for e in range(3):
                        t = 9 * a + 3 * b + e
                        t = taps - 1 - t if v else t
                        parts.append(picked[t * coils:(t + 1) * coils, (2 * v + po) * inputs:(2 * v + po + 1) * inputs])
                    first = (((v * 3 + b) * 3 + a) * 2 + po) * coils
                    wf[first:first + coils, :] = jnp.concatenate(parts, 1)
    target[...] = wf[...].astype(jnp.bfloat16)


def split(x):
    hi = x.astype(jnp.bfloat16)
    return hi, (x - hi.astype(jnp.float32)).astype(jnp.bfloat16)


def body(sizes, row, measured, mask, kernel, out, x, xh, xl, wf, wh, wl, r1, r2, rm,
         g_send, g_recv, z_send, z_recv, k_send, k_recv, m_send, m_recv):
    nz, nc = sizes
    planes, rows, lanes = measured.shape
    wide = lanes + LANES
    z, c, h = lax.axis_index("kz"), lax.axis_index("coil"), lax.axis_index("kx")
    mirror = {"kz": nz - 1 - z, "kx": 1 - h}

    barrier = pltpu.get_barrier_semaphore()
    for d in range(1, nc):
        pl.semaphore_signal(barrier, inc=1, device_id={"coil": lax.rem(c + d, nc)}, device_id_type=MESH)
    pl.semaphore_signal(barrier, inc=1, device_id={"kx": 1 - h}, device_id_type=MESH)
    pl.semaphore_signal(barrier, inc=1, device_id=mirror, device_id_type=MESH)

    for d in (1, nz - 1):
        pl.semaphore_signal(barrier, inc=1, device_id={"kz": lax.rem(z + d, nz)}, device_id_type=MESH)
    pl.semaphore_wait(barrier, nc + 3)

    lane = lax.broadcasted_iota(jnp.int32, (1, wide), 1)
    edge = lane - lanes - h * (LANES - row)
    keep = (lane < lanes) | ((edge >= 0) & (edge < row))
    column = lax.rem(lane, row)
    after, before = column > 0, column < row - 1
    flip = (lax.broadcasted_iota(jnp.int32, (LANES, LANES), 0)
            + lax.broadcasted_iota(jnp.int32, (LANES, LANES), 1) == LANES - 1)
    flip = flip.astype(jnp.float32).astype(jnp.bfloat16)

    def remote(src, dst, send, recv, device):
        return pltpu.make_async_remote_copy(
            src_ref=src, dst_ref=dst, send_sem=send, recv_sem=recv, device_id=device, device_id_type=MESH)

    slots = planes + 2

    def combine(step, k):
        sampled = mask[k] == 1
        hi, lo = split(rm[step, k])
        parts = []
        for q in range(lanes // LANES):
            s = slice(lanes - (q + 1) * LANES, lanes - q * LANES)
            parts.append(jnp.dot(hi[:, s], flip, preferred_element_type=jnp.float32)
                         + jnp.dot(lo[:, s], flip, preferred_element_type=jnp.float32))
        return jnp.where(sampled, measured[k], r1[k] + jnp.concatenate(parts, 1))

    def gather(step, slot, d):
        own = x.at[step, slot, c, :, pl.ds(0, lanes)]
        return remote(own, own, g_send.at[step, d - 1, slot], g_recv.at[step, d - 1, slot],
                      {"coil": lax.rem(c + d, nc)})

    def outer(step):
        down = remote(x.at[step, 1, c, :, pl.ds(0, lanes)], x.at[step, planes + 1, c, :, pl.ds(0, lanes)],
                      z_send.at[step, 0], z_recv.at[step, 0], {"kz": lax.max(z - 1, 0)})
        up = remote(x.at[step, planes, c, :, pl.ds(0, lanes)], x.at[step, 0, c, :, pl.ds(0, lanes)],
                    z_send.at[step, 1], z_recv.at[step, 1], {"kz": lax.min(z + 1, nz - 1)})
        return down, up

    def side(step, slot):
        near = pl.multiple_of((1 - h) * (lanes - LANES), LANES)
        return remote(x.at[step, slot, :, :, pl.ds(near, LANES)], x.at[step, slot, :, :, pl.ds(lanes, LANES)],
                      k_send.at[step, slot], k_recv.at[step, slot], {"kx": 1 - h})

    def send(step, k):
        return remote(r2.at[step, k], rm.at[step, planes - 1 - k], m_send.at[step, k],
                      m_recv.at[step, planes - 1 - k], mirror)

    def receive(step, k):
        remote(r2.at[step, planes - 1 - k], rm.at[step, k], m_send.at[step, planes - 1 - k],
               m_recv.at[step, k], mirror).wait_recv()

    def start_outer(step):
        down, up = outer(step)

        @pl.when(z > 0)
        def _():
            down.start()

        @pl.when(z < nz - 1)
        def _():
            up.start()

    def wait_outer(step):
        down, up = outer(step)

        @pl.when(z > 0)
        def _():
            down.wait_send()
            up.wait_recv()

        @pl.when(z < nz - 1)
        def _():
            up.wait_send()
            down.wait_recv()

    def start_gather(step, n):
        for d in range(1, nc):
            gather(step, order(n, slots, step), d).start()

    def wait_gather(step, n):
        slot = order(n, slots, step)
        for d in range(1, nc):
            gather(step, slot, d).wait_recv()
        side(step, slot).start()

    def divide(step, n):
        slot = order(n, slots, step)
        side(step, slot).wait_recv()
        value = x[step, slot].reshape(nc * rows, wide)
        xh[slot], xl[slot] = split(jnp.where(keep, value, 0.0))

    def convolve(step, n):
        k = order(n, slots, step) - 1
        hi = xh[pl.ds(k, 3)].reshape(-1, wide)
        lo = xl[pl.ds(k, 3)].reshape(-1, wide)
        results = []
        for v in (1, 0):
            w = slice(v * 9 * rows, (v + 1) * 9 * rows)
            p = (jnp.dot(wh[w], hi, preferred_element_type=jnp.float32)
                 + jnp.dot(wh[w], lo, preferred_element_type=jnp.float32)
                 + jnp.dot(wl[w], hi, preferred_element_type=jnp.float32))
            total = None
            for b in (1, 0, 2):
                t = p[(3 * b + 1) * rows:(3 * b + 2) * rows]
                t = t + pltpu.roll(p[3 * b * rows:(3 * b + 1) * rows], row, 1)
                t = t + pltpu.roll(p[(3 * b + 2) * rows:(3 * b + 3) * rows], wide - row, 1)
                if b == 0:
                    t = jnp.where(after, pltpu.roll(t, 1, 1), 0.0)
                if b == 2:
                    t = jnp.where(before, pltpu.roll(t, wide - 1, 1), 0.0)
                total = t if total is None else total + t
            results.append(total[:, :lanes])
            if v:
                r2[step, k] = results[0]
        r1[k] = results[1]
        send(step, k).start()

    for step in range(ITERS):
        @pl.when(z == 0)
        def _():
            x[step, 0, c, :, :lanes] = jnp.zeros((rows, lanes), jnp.float32)

        @pl.when(z == nz - 1)
        def _():
            x[step, planes + 1, c, :, :lanes] = jnp.zeros((rows, lanes), jnp.float32)

    def first(k, _):
        x[0, k + 1, c, :, :lanes] = jnp.where(mask[k] == 1, measured[k], 0.0)
        return 0

    lax.fori_loop(0, planes, first, 0)
    start_outer(0)

    def first_gather(n, _):
        start_gather(0, n)
        return 0

    lax.fori_loop(0, planes, first_gather, 0)
    place_weights(kernel, nc, wf, wh, 0)
    wait_outer(0)
    lax.fori_loop(planes, slots, first_gather, 0)
    for n in (0, 1):
        wait_gather(0, n)
    place_weights(kernel, nc, wf, wl, 1)

    def stage(n, _):
        @pl.when(n < slots + 2)
        def _():
            divide(0, n - 2)

        @pl.when(n >= 4)
        def _():
            convolve(0, n - 4)

        @pl.when(n < slots)
        def _():
            wait_gather(0, n)

        return 0

    lax.fori_loop(2, planes + 4, stage, 0)

    for step in range(1, ITERS):
        def again(n, _):
            @pl.when(n < planes)
            def _():
                k = order(n, slots, step) - 1
                receive(step - 1, k)
                x[step, k + 1, c, :, :lanes] = combine(step - 1, k)

            @pl.when((n >= 3) & (n < planes + 3))
            def _():
                divide(step, n - 3)

            @pl.when(n == planes - 1)
            def _():
                start_outer(step)

            @pl.when(n < planes)
            def _():
                start_gather(step, n)

            @pl.when(n == planes + 1)
            def _():
                wait_outer(step)
                start_gather(step, planes)
                start_gather(step, planes + 1)

            @pl.when(n >= 5)
            def _():
                convolve(step, n - 5)

            @pl.when((n >= 2) & (n < planes + 2))
            def _():
                wait_gather(step, n - 2)

            return 0

        lax.fori_loop(0, planes + 3, again, 0)
        for n in (planes, planes + 1):
            wait_gather(step, n)

        def rest(n, _):
            divide(step, n + 2)
            convolve(step, n)
            return 0

        lax.fori_loop(planes - 2, planes, rest, 0)

    def last(n, _):
        k = order(n, slots, ITERS) - 1
        receive(ITERS - 1, k)
        out[k] = combine(ITERS - 1, k)
        return 0

    lax.fori_loop(0, planes, last, 0)

    for step in range(ITERS):
        def sent(slot, _):
            for d in range(1, nc):
                gather(step, slot, d).wait_send()
            side(step, slot).wait_send()
            return 0

        lax.fori_loop(0, slots, sent, 0)

        def mirrored(k, _):
            send(step, k).wait_send()
            return 0

        lax.fori_loop(0, planes, mirrored, 0)


def on_device(sizes, measured, mask, kernel):
    nz, nc = sizes
    _, coils, depth_x, planes, row = measured.shape
    rows, lanes = 2 * coils, depth_x * row
    wide = lanes + LANES
    flat = measured.transpose(3, 0, 1, 2, 4).reshape(planes, rows, lanes)
    sampled = mask.transpose(1, 0, 2).reshape(planes, 1, lanes)
    weights = (18 * rows, 3 * nc * rows)
    vmem = pl.BlockSpec(memory_space=pltpu.VMEM)
    dma = pltpu.SemaphoreType.DMA
    result = pl.pallas_call(
        functools.partial(body, sizes, row),
        out_shape=jax.ShapeDtypeStruct((planes, rows, lanes), jnp.float32),
        in_specs=[vmem] * 3,
        out_specs=vmem,
        scratch_shapes=[
            pltpu.VMEM((ITERS, planes + 2, nc, rows, wide), jnp.float32),
            pltpu.VMEM((planes + 2, nc * rows, wide), jnp.bfloat16),
            pltpu.VMEM((planes + 2, nc * rows, wide), jnp.bfloat16),
            pltpu.VMEM(weights, jnp.float32),
            pltpu.VMEM(weights, jnp.bfloat16),
            pltpu.VMEM(weights, jnp.bfloat16),
            pltpu.VMEM((planes, rows, lanes), jnp.float32),
            pltpu.VMEM((ITERS, planes, rows, lanes), jnp.float32),
            pltpu.VMEM((ITERS, planes, rows, lanes), jnp.float32),
            dma((ITERS, nc - 1, planes + 2)), dma((ITERS, nc - 1, planes + 2)),
            dma((ITERS, 2)), dma((ITERS, 2)),
            dma((ITERS, planes + 2)), dma((ITERS, planes + 2)),
            dma((ITERS, planes)), dma((ITERS, planes)),
        ],
        compiler_params=pltpu.CompilerParams(collective_id=0, has_side_effects=True),
    )(flat, sampled, kernel)
    result = result.reshape(planes, 2, coils, depth_x, row)
    return result.transpose(1, 2, 3, 0, 4)


def solution(mesh):
    placed = (
        P(None, ("grp", "coil"), "kx", "kz", None),
        P(("grp", "kx"), "kz", None),
        P(None, None, "coil", None),
    )
    return jax.shard_map(
        functools.partial(on_device, (mesh.shape["kz"], mesh.shape["coil"])),
        mesh=mesh,
        in_specs=placed,
        out_specs=P(None, ("grp", "coil"), "kx", "kz", None),
        check_vma=False,
    )
```

profile of v0, /device:TPU:9, one launch (start us, length us, event | category | flops | bytes accessed | tf_op | source)
XLA Modules:
  0.0 72.8 jit_solution(5729948511999352936)
XLA Ops:
  0.0 0.9 %copy.5 = s32[8,16,32]{2,1,0:T(8,128)S(1)} copy(s32[8,16,32]{2,0,1:T(8,128)} %bitcast.8) | data formatting | bytes 32768 | tf_op jit(solution)/shard_map/transpose | solution.py:310
  0.9 0.7 reshape.10.mask
  1.5 2.0 %copy.4 = f32[8,2,16,16,32]{4,3,2,1,0:T(8,128)S(1)} copy(f32[8,2,16,16,32]{4,0,3,2,1:T(8,128)} %bitcast.7) | data formatting | bytes 1048576 | tf_op jit(solution)/shard_map/transpose | solution.py:309
  3.5 1.6 %reshape.9.measured = f32[8,32,512]{2,1,0:T(8,128)} reshape(f32[8,2,16,16,32]{4,3,2,1,0:T(8,128)S(1)} %copy.4) | data formatting | bytes 1048576 | tf_op jit(solution)/shard_map/reshape | solution.py:309
  5.1 63.5 %shard_map.37 = f32[8,32,512]{2,1,0:T(8,128)} custom-call(f32[8,32,512]{2,1,0:T(8,128)} %reshape.9.measured, s32[8,1,512]{2,1,0:T(1,128)} %reshape.10.mask, f32[27,2,16,64]{3,2,1,0:T(8,128)} %kernel.1), custom_call_target="tpu_custom_call" | custom-call | tf_op jit(solution)/shard_map/pallas_call | solution.py:314
  68.6 1.6 %reshape.11 = f32[8,2,16,16,32]{4,3,2,1,0:T(8,128)S(1)} reshape(f32[8,32,512]{2,1,0:T(8,128)} %shard_map.37) | data formatting | bytes 1048576 | tf_op jit(solution)/shard_map/reshape | solution.py:336
  70.2 2.5 %copy.8 = f32[8,2,16,16,32]{4,0,3,2,1:T(8,128)} copy(f32[8,2,16,16,32]{4,3,2,1,0:T(8,128)S(1)} %reshape.11) | data formatting | bytes 1048576 | tf_op jit(solution)/shard_map/reshape | solution.py:336
where the time goes:
time: 73.2 us; the launch traced here: 72.8 us
  Pallas kernels  63.5 us (87%)
  local copies, waits for them, and re-layouts  9.3 us (13%)
    pallas_call x1, Pallas kernels, on_device(): pl.pallas_call(functools.partial(body, sizes, row), out_shape=jax.ShapeDt...  63.5 us
    reshape x2, local copies, waits for them, and re-layouts, on_device(): result = result.reshape(planes, 2, coils, depth_x, row)  4.17 us
    transpose x1, local copies, waits for them, and re-layouts, on_device(): flat = measured.transpose(3, 0, 1, 2, 4).reshape(planes, rows, lanes)  2 us
    reshape x1, local copies, waits for them, and re-layouts, on_device(): flat = measured.transpose(3, 0, 1, 2, 4).reshape(planes, rows, lanes)  1.58 us

commit v1 on v0

v1 whole, which is shorter than its diff:
```python
import functools

import jax
import jax.numpy as jnp
from jax import lax
from jax.experimental import pallas as pl
from jax.experimental.pallas import tpu as pltpu
from jax.sharding import PartitionSpec as P

ITERS = 2
TAPS = 27
CHUNK = 2
MESH = pl.DeviceIdType.MESH
F32, BF16 = jnp.float32, jnp.bfloat16
NT = (((1,), (1,)), ((), ()))


def split(x):
    hi = x.astype(BF16)
    return hi, (x - hi.astype(F32)).astype(BF16)


def reversal(n):
    i = lax.broadcasted_iota(jnp.int32, (n, n), 0) + lax.broadcasted_iota(jnp.int32, (n, n), 1)
    return jnp.where(i == n - 1, 1.0, 0.0).astype(BF16)


def body(sizes, measured, mask, kernel, out, hd, hm, rb, mb, kb, w, st, mt, xb, hz, hg, hq, ob, fr,
         s_send, s_recv, v_send, v_recv, k_send, k_recv, m_send, m_recv, h_send, h_recv, os_send, os_recv, ov_send, ov_recv):
    nz, nc = sizes
    _, coils, depth_x, planes, row = measured.shape
    half = nz // 2
    groups = 2 * nc
    g = depth_x // groups
    lanes = g * row
    band = nc * coils
    chans = 4 * band
    wide = 2 * chans

    z, c, h = lax.axis_index("kz"), lax.axis_index("coil"), lax.axis_index("kx")
    side = lax.div(z, half)
    far = nz - 1 - z
    eq = lax.rem(side + h + 1, 2)

    def pos(zz, cx):
        turn = lax.rem(lax.min(zz, nz - 1 - zz), 2)
        return turn * (nc - 1 - cx) + (1 - turn) * cx

    cc = pos(z, c)

    def own_group(at):
        return eq * at + (1 - eq) * (groups - 1 - at)

    def coil_at(d):
        return lax.rem(c + d, nc)

    def neighbour(dz, dc):
        zt = z + dz
        good = (zt >= 0) & (zt < nz)
        zt = lax.max(lax.min(zt, nz - 1), 0)
        over = lax.rem(lax.div(zt, half) + side, 2)
        inter = lax.div(cc + 1, nc) if dc > 0 else 0
        core = 1 - lax.min(cc, 1) if dc < 0 else 0
        if dc < 0:
            good = good & ((side == 1) | (cc > 0))
        flip = lax.rem(over + inter, 2)
        tz = flip * (nz - 1 - zt) + (1 - flip) * zt
        tcc = cc + dc - inter + core
        th = lax.rem(h + flip + core, 2)
        sz, sc = (dz + 1) // 2, (dc + 1) // 2
        stay = inter + core
        tsz = flip * sz + (1 - flip) * (1 - sz)
        tsc = stay * sc + (1 - stay) * (1 - sc)
        alone = (over * core == 1) & good
        return dict(good=good & jnp.logical_not(alone), alone=alone, flip=flip,
                    device={"kz": tz, "coil": pos(tz, tcc), "kx": th}, sz=sz, sc=sc, tsz=tsz, tsc=tsc)

    dirs = [(dz, dc) for dz in (-1, 0, 1) for dc in (-1, 0, 1) if dz or dc]
    near = {d: neighbour(*d) for d in dirs}
    maybe_alone = [(-1, -1), (1, -1)]

    barrier = pltpu.get_barrier_semaphore()
    for d in range(nc):
        if d:
            pl.semaphore_signal(barrier, inc=1, device_id={"coil": coil_at(d)}, device_id_type=MESH)
        pl.semaphore_signal(barrier, inc=1, device_id={"kz": far, "coil": coil_at(d), "kx": 1 - h}, device_id_type=MESH)
    count = 2 * nc - 1
    for d in dirs:
        @pl.when(near[d]["good"])
        def _():
            pl.semaphore_signal(barrier, inc=1, device_id=near[d]["device"], device_id_type=MESH)
        count = count + near[d]["good"].astype(jnp.int32)
    pl.semaphore_wait(barrier, count)

    def remote(src, dst, send, recv, device):
        return pltpu.make_async_remote_copy(
            src_ref=src, dst_ref=dst, send_sem=send, recv_sem=recv, device_id=device, device_id_type=MESH)

    def same_copy(d):
        return remote(hd.at[own_group(pos(z, coil_at(d)))], rb.at[:, :, 0, c], s_send.at[d], s_recv.at[d],
                      {"coil": coil_at(d)})

    def far_copy(d):
        return remote(hd.at[groups - 1 - own_group(pos(z, coil_at(d)))], rb.at[:, :, 1, c], v_send.at[d], v_recv.at[d],
                      {"kz": far, "coil": coil_at(d), "kx": 1 - h})

    def kernel_copy(d):
        return remote(kb.at[c], kb.at[c], k_send.at[d], k_recv.at[d], {"coil": coil_at(d)})

    mask_copy = remote(hm.at[groups - 1 - own_group(cc)], mb.at[1], m_send, m_recv,
                       {"kz": far, "kx": 1 - h})

    hd_rows = hd.reshape(groups * planes * 2 * coils, lanes)
    fr_rows = fr.reshape(groups * planes * 2 * coils, lanes)

    def pack(m):
        keep = jnp.concatenate([mask[m * g + i] for i in range(g)], 1) == 1
        hm[m] = jnp.where(keep, 1.0, 0.0)
        for ri in range(2):
            for coil in range(coils):
                value = jnp.concatenate([measured[ri, coil, m * g + i] for i in range(g)], 1)
                hd_rows[pl.ds(m * planes * 2 * coils + ri * coils + coil, planes, stride=2 * coils), :] = jnp.where(keep, value, 0.0)

    def pack_far(d, _):
        pack(groups - 1 - own_group(pos(z, coil_at(d))))
        far_copy(d).start()
        return 0

    lax.fori_loop(0, nc, pack_far, 0)
    mask_copy.start()
    kb[c] = jnp.concatenate([kernel[:, 0], kernel[:, 1]], 2)
    for d in range(1, nc):
        kernel_copy(d).start()

    def pack_same(d, _):
        pack(own_group(pos(z, coil_at(d))))

        @pl.when(d > 0)
        def _():
            same_copy(d).start()

        return 0

    lax.fori_loop(0, nc, pack_same, 0)
    mine = own_group(cc)
    rb[:, :, 0, c] = hd[mine]
    mb[0] = hm[mine]

    for step in range(ITERS):
        for sz in range(2):
            @pl.when(jnp.logical_not(near[(2 * sz - 1, 0)]["good"]))
            def _():
                hz[step, sz] = jnp.zeros(hz.shape[2:], F32)
            for sc in range(2):
                @pl.when(jnp.logical_not(near[(2 * sz - 1, 2 * sc - 1)]["good"]))
                def _():
                    hq[step, sz, sc] = jnp.zeros(hq.shape[3:], F32)
        @pl.when(jnp.logical_not(near[(0, -1)]["good"]))
        def _():
            hg[step, 0] = jnp.zeros(hg.shape[2:], F32)

    for d in range(1, nc):
        kernel_copy(d).wait_recv()
    lane = lax.broadcasted_iota(jnp.int32, (1, chans), 1)
    first = lax.rem(lax.div(lane, band), 2) == 0
    upper = lane >= 2 * band

    def swap(x):
        return jnp.where(first, pltpu.roll(x, chans - band, 1), pltpu.roll(x, band, 1))

    def sign(s):
        return jnp.where(upper, jnp.where(first, s, -s), 1.0)

    def weights(t, _):
        plain = kb[:, t].reshape(band, chans)
        turned = swap(kb[:, TAPS - 1 - t].reshape(band, chans))
        rows = (plain * sign(-1.0), turned * sign(1.0),
                pltpu.roll(plain, 2 * band, 1) * sign(1.0), pltpu.roll(turned, 2 * band, 1) * sign(-1.0))
        for n, value in enumerate(rows):
            hi, lo = split(value)
            w[t, n * band:(n + 1) * band, :] = jnp.concatenate([hi, hi], 1)
            w[t, chans + n * band:chans + (n + 1) * band, :] = jnp.concatenate([lo, jnp.zeros_like(lo)], 1)
        return 0

    lax.fori_loop(0, TAPS, weights, 0)

    turn = reversal(lanes)
    eye = (lax.broadcasted_iota(jnp.int32, (lanes, lanes), 0) == lax.broadcasted_iota(jnp.int32, (lanes, lanes), 1))
    both = jnp.concatenate([jnp.where(eye, 1.0, 0.0).astype(BF16), turn], 1)
    is_state = lax.rem(lax.div(lax.broadcasted_iota(jnp.int32, (chans, 1), 0), band), 2) == 0

    def put(step, x, k, r, n, m):
        rows = n * m * row
        j = lax.rem(lax.broadcasted_iota(jnp.int32, (rows, 1), 0), row)
        for b in range(3):
            y = x
            if b == 0:
                y = jnp.where(j > 0, pltpu.roll(x, 1, 0), 0.0)
            if b == 2:
                y = jnp.where(j < row - 1, pltpu.roll(x, rows - 1, 0), 0.0)
            hi, lo = split(y)
            xb[step, b, pl.ds(k, n), pl.ds(r, m)] = jnp.concatenate([hi, lo], 1).reshape(n, m, row, wide)

    for d in range(nc):
        if d:
            same_copy(d).wait_recv()
        far_copy(d).wait_recv()
    mask_copy.wait_recv()

    def transpose_in(k, _):
        kv = planes - 1 - k
        xs, xv = rb[k].reshape(chans, lanes), rb[kv].reshape(chans, lanes)
        cat = jnp.concatenate([jnp.where(is_state, xs, 0.0), jnp.where(is_state, 0.0, xv)], 1)
        hi, lo = split(cat)
        ms = jnp.broadcast_to(mb[0, pl.ds(k, 1)], (chans, lanes))
        mv = jnp.broadcast_to(mb[1, pl.ds(kv, 1)], (chans, lanes))
        mk = jnp.concatenate([jnp.where(is_state, ms, 0.0), jnp.where(is_state, 0.0, mv)], 1).astype(BF16)
        t = lax.dot_general(both, jnp.concatenate([hi, lo, mk], 0), NT, preferred_element_type=F32)
        x = t[:, :chans] + t[:, chans:2 * chans]
        mt[k] = t[:, 2 * chans:]
        st[0, k] = x.reshape(g, row, chans)
        put(0, x, k + 1, 1, 1, g)
        return 0

    lax.fori_loop(0, planes, transpose_in, 0)

    def edge(sc, inner):
        up = eq * sc + (1 - eq) * (1 - sc)
        return up * (g - 1) if inner else up * (g + 1)

    def halo_copy(step, d):
        v = near[d]
        n = dirs.index(d)
        plane = planes - 1 if d[0] > 0 else 0
        sem = 0
        if d[1] == 0:
            src, dst = st.at[step, plane], hz.at[step, v["tsz"]]
            sem = v["tsz"]
        elif d[0] == 0:
            src, dst = st.at[step, :, edge(v["sc"], True)], hg.at[step, v["tsc"]]
            sem = 2 + v["tsc"]
        else:
            src, dst = st.at[step, plane, edge(v["sc"], True)], hq.at[step, v["tsz"], v["tsc"]]
            sem = 4 + 2 * v["tsz"] + v["tsc"]
        return remote(src, dst, h_send.at[step, n], h_recv.at[step, sem], v["device"])

    def halo_land(step, d):
        v = near[d]
        if d[1] == 0:
            return hz.at[step, v["sz"]], v["sz"]
        if d[0] == 0:
            return hg.at[step, v["sc"]], 2 + v["sc"]
        return hq.at[step, v["sz"], v["sc"]], 4 + 2 * v["sz"] + v["sc"]

    order = [(0, 1), (0, -1), (1, 0), (-1, 0), (1, 1), (-1, 1), (1, -1), (-1, -1)]

    def start_halo(step):
        for d in order:
            @pl.when(near[d]["good"])
            def _():
                halo_copy(step, d).start()
        for d in maybe_alone:
            @pl.when(near[d]["alone"])
            def _():
                v = near[d]
                hq[step, v["sz"], v["sc"]] = st[step, planes - 1 if d[0] > 0 else 0, edge(v["sc"], True)]

    def flipped(x, rows):
        hi, lo = split(x)
        y = jnp.dot(reversal(rows), jnp.concatenate([hi, lo], 1), preferred_element_type=F32)
        return swap(y[:, :chans] + y[:, chans:])

    def take_halo(step):
        for d in order[2:4] + order[:2] + order[4:]:
            v = near[d]
            buf, sem = halo_land(step, d)

            @pl.when(v["good"])
            def _():
                remote(buf, buf, h_send.at[step, dirs.index(d)], h_recv.at[step, sem], v["device"]).wait_recv()

            n = planes if d[0] == 0 else 1
            m = g if d[1] == 0 else 1
            rows = n * m * row
            x = buf[...].reshape(rows, chans)
            x = jnp.where(v["flip"] == 1, flipped(x, rows), x)
            k = 1 if d[0] == 0 else (planes + 1 if d[0] > 0 else 0)
            r = 1 if d[1] == 0 else edge(v["sc"], False)
            put(step, x, k, r, n, m)

    def convolve(step, k):
        x = jnp.concatenate([xb[step, (t // 3) % 3, pl.ds(k + t % 3, CHUNK), pl.ds(t // 9, g)].reshape(CHUNK * lanes, wide)
                             for t in range(TAPS)], 1)
        p = lax.dot_general(x, jnp.concatenate([w[t] for t in range(TAPS)], 1), NT, preferred_element_type=F32)
        return p[:, :chans] + p[:, chans:]

    start_halo(0)
    take_halo(0)

    for step in range(ITERS - 1):
        def iterate(n, _):
            result = convolve(step, n * CHUNK)
            for i in range(CHUNK):
                k = n * CHUNK + i
                x = jnp.where(mt[k] > 0.5, st[0, k].reshape(lanes, chans), result[i * lanes:(i + 1) * lanes])
                st[step + 1, k] = x.reshape(g, row, chans)
                put(step + 1, x, k + 1, 1, 1, g)
            return 0

        lax.fori_loop(0, planes // CHUNK, iterate, 0)
        start_halo(step + 1)
        take_halo(step + 1)

    def same_back(d, n):
        k = pl.ds(n * CHUNK, CHUNK)
        return remote(ob.at[k, :, 0, coil_at(d)], fr.at[mine, k], os_send.at[d, n], os_recv.at[d, n],
                      {"coil": coil_at(d)})

    def far_back(d, n):
        k = pl.ds(planes - (n + 1) * CHUNK, CHUNK)
        return remote(ob.at[k, :, 1, coil_at(d)], fr.at[groups - 1 - mine, k], ov_send.at[d, n], ov_recv.at[d, n],
                      {"kz": far, "coil": coil_at(d), "kx": 1 - h})

    turn2 = jnp.concatenate([turn, turn], 1)

    def finish(n, _):
        result = convolve(ITERS - 1, n * CHUNK)
        for i in range(CHUNK):
            k = n * CHUNK + i
            r = result[i * lanes:(i + 1) * lanes]
            hi, lo = split(r)
            back = jnp.dot(turn2, jnp.concatenate([hi, lo], 0), preferred_element_type=F32)
            y = jnp.where(first, r, back).T.reshape(2, 2, nc, coils, lanes)
            ob[k, :, 0] = y[:, 0]
            ob[planes - 1 - k, :, 1] = y[:, 1]
        for d in range(nc):
            far_back(d, n).start()
        for d in range(1, nc):
            same_back(d, n).start()
        return 0

    lax.fori_loop(0, planes // CHUNK, finish, 0)
    fr[mine] = ob[:, :, 0, c]

    def unpack(m):
        keep = hm[m] > 0.5
        for ri in range(2):
            for coil in range(coils):
                at = pl.ds(m * planes * 2 * coils + ri * coils + coil, planes, stride=2 * coils)
                value = jnp.where(keep, hd_rows[at, :], fr_rows[at, :])
                for i in range(g):
                    out[ri, coil, m * g + i] = value[:, i * row:(i + 1) * row]

    def landed(send, recv, m, d, n):
        k = pl.ds(n * CHUNK, CHUNK)
        remote(ob.at[k, :, 0, 0], fr.at[m, k], send.at[d, n], recv.at[d, n], {"coil": coil_at(1)}).wait_recv()

    def same_home(d, _):
        m = own_group(pos(z, lax.rem(c + nc - d, nc)))

        @pl.when(d > 0)
        def _():
            for n in range(planes // CHUNK):
                landed(os_send, os_recv, m, d, n)

        unpack(m)
        return 0

    def far_home(d, _):
        m = groups - 1 - own_group(pos(z, lax.rem(c + nc - d, nc)))
        for n in range(planes // CHUNK):
            landed(ov_send, ov_recv, m, d, n)
        unpack(m)
        return 0

    lax.fori_loop(0, nc, same_home, 0)
    lax.fori_loop(0, nc, far_home, 0)

    for d in range(nc):
        far_copy(d).wait_send()
        if d:
            same_copy(d).wait_send()
            kernel_copy(d).wait_send()
        for n in range(planes // CHUNK):
            far_back(d, n).wait_send()
            if d:
                same_back(d, n).wait_send()
    mask_copy.wait_send()
    for step in range(ITERS):
        for d in dirs:
            @pl.when(near[d]["good"])
            def _():
                halo_copy(step, d).wait_send()


def on_device(sizes, measured, mask, kernel):
    nz, nc = sizes
    _, coils, depth_x, planes, row = measured.shape
    groups = 2 * nc
    g = depth_x // groups
    lanes = g * row
    chans = 4 * nc * coils
    parts = planes // CHUNK
    vmem = pl.BlockSpec(memory_space=pltpu.VMEM)
    dma = pltpu.SemaphoreType.DMA
    return pl.pallas_call(
        functools.partial(body, sizes),
        out_shape=jax.ShapeDtypeStruct(measured.shape, F32),
        in_specs=[vmem] * 3,
        out_specs=vmem,
        scratch_shapes=[
            pltpu.VMEM((groups, planes, 2, coils, lanes), F32),
            pltpu.VMEM((groups, planes, lanes), F32),
            pltpu.VMEM((planes, 2, 2, nc, coils, lanes), F32),
            pltpu.VMEM((2, planes, lanes), F32),
            pltpu.VMEM((nc, TAPS, coils, chans), F32),
            pltpu.VMEM((TAPS, 2 * chans, 2 * chans), BF16),
            pltpu.VMEM((ITERS, planes, g, row, chans), F32),
            pltpu.VMEM((planes, lanes, chans), F32),
            pltpu.VMEM((ITERS, 3, planes + 2, g + 2, row, 2 * chans), BF16),
            pltpu.VMEM((ITERS, 2, g, row, chans), F32),
            pltpu.VMEM((ITERS, 2, planes, row, chans), F32),
            pltpu.VMEM((ITERS, 2, 2, row, chans), F32),
            pltpu.VMEM((planes, 2, 2, nc, coils, lanes), F32),
            pltpu.VMEM((groups, planes, 2, coils, lanes), F32),
            dma((nc,)), dma((nc,)), dma((nc,)), dma((nc,)), dma((nc,)), dma((nc,)), dma, dma,
            dma((ITERS, 8)), dma((ITERS, 8)),
            dma((nc, parts)), dma((nc, parts)), dma((nc, parts)), dma((nc, parts)),
        ],
        compiler_params=pltpu.CompilerParams(collective_id=0, has_side_effects=True, vmem_limit_bytes=56 << 20),
    )(measured, mask, kernel)


def solution(mesh):
    placed = (
        P(None, ("grp", "coil"), "kx", "kz", None),
        P(("grp", "kx"), "kz", None),
        P(None, None, "coil", None),
    )
    return jax.shard_map(
        functools.partial(on_device, (mesh.shape["kz"], mesh.shape["coil"])),
        mesh=mesh,
        in_specs=placed,
        out_specs=P(None, ("grp", "coil"), "kx", "kz", None),
        check_vma=False,
    )
```

time: 73.2 us -> 62.2 us (0.85)
  local copies, waits for them, and re-layouts: 9.3 us -> 3.14 us
  Pallas kernels: 63.5 us -> 58.9 us
    reshape x4 -> x0, local copies, waits for them, and re-layouts: 6.45 us -> none  [the longest x2 4.17 us: on_device(): result = result.reshape(planes, 2, coils, depth_x, row)]
    pallas_call x1, Pallas kernels: 63.5 us -> 58.9 us  [on_device(): pl.pallas_call(functools.partial(body, sizes), out_shape=jax.ShapeDtypeSt...]
    unnamed x0 -> x1, local copies, waits for them, and re-layouts: none -> 3.14 us
    transpose x2 -> x0, local copies, waits for them, and re-layouts: 2.85 us -> none  [the longest x1 2 us: on_device(): flat = measured.transpose(3, 0, 1, 2, 4).reshape(planes, rows, lanes)]
where the time goes in v1:
time: 62.2 us; the launch traced here: 62 us
  Pallas kernels  58.9 us (95%)
  local copies, waits for them, and re-layouts  3.14 us (5%)
    pallas_call x1, Pallas kernels, on_device(): pl.pallas_call(functools.partial(body, sizes), out_shape=jax.ShapeDtypeSt...  58.9 us
    unnamed x1, local copies, waits for them, and re-layouts  3.14 us

profile of v1, /device:TPU:9, one launch (start us, length us, event | category | flops | bytes accessed | tf_op | source)
XLA Modules:
  0.0 62.0 jit_solution(11044437811614457720)
XLA Ops:
  0.0 58.9 %shard_map.37 = f32[2,16,16,8,32]{4,3,2,1,0:T(8,128)} custom-call(f32[2,16,16,8,32]{4,3,2,1,0:T(8,128)} %measured.1, s32[16,8,32]{2,1,0:T(8,128)} %mask.1, f32[27,2,16,64]{3,2,1,0:T(8,128)} %kernel.1), custom_call_target="tpu_custom_call" | custom-call | tf_op jit(solution)/shard_map/pallas_call | solution.py:406
  58.9 3.1 %copy.5 = f32[2,16,16,8,32]{4,3,2,1,0:T(8,128)} copy(f32[2,16,16,8,32]{4,3,2,1,0:T(8,128)} %shard_map.37) | data formatting | bytes 1048576

commit v2 on v1

v2 whole, which is shorter than its diff:
```python
import functools

import jax
import jax.numpy as jnp
from jax import lax
from jax.experimental import pallas as pl
from jax.experimental.pallas import tpu as pltpu
from jax.sharding import PartitionSpec as P

ITERS = 2
TAPS = 27
CHUNK = 2
MESH = pl.DeviceIdType.MESH
F32, BF16 = jnp.float32, jnp.bfloat16
NT = (((1,), (1,)), ((), ()))


def split(x):
    hi = x.astype(BF16)
    return hi, (x - hi.astype(F32)).astype(BF16)


def reversal(n):
    i = lax.broadcasted_iota(jnp.int32, (n, n), 0) + lax.broadcasted_iota(jnp.int32, (n, n), 1)
    return jnp.where(i == n - 1, 1.0, 0.0).astype(BF16)


def body(sizes, measured_hbm, mask_hbm, kernel_hbm, out, measured, mask, kernel, hd, hm, rb, mb, kb, w, st, mt, xb, hz, hg, hq, acc, ob, fr,
         in_sem, s_send, s_recv, v_send, v_recv, k_send, k_recv, f_send, f_recv, m_send, m_recv,
         hz_send, hz_recv, hg_send, hg_recv, hq_send, hq_recv, os_send, os_recv, ov_send, ov_recv):
    nz, nc = sizes
    _, coils, depth_x, planes, row = measured.shape
    half = nz // 2
    groups = 2 * nc
    g = depth_x // groups
    lanes = g * row
    band = nc * coils
    chans = 4 * band
    wide = 2 * chans
    parts = planes // CHUNK

    z, c, h = lax.axis_index("kz"), lax.axis_index("coil"), lax.axis_index("kx")
    side = lax.div(z, half)
    far = nz - 1 - z

    def owner(tz, thalf, place):
        q = lax.rem(thalf + lax.div(tz, half), 2)
        return {"kz": tz, "coil": q * (nc // 2) + lax.div(place, 2), "kx": lax.rem(place, 2)}

    kxh = lax.rem(lax.div(c, nc // 2) + side, 2)
    cc = lax.rem(c, nc // 2) * 2 + h
    stays = kxh == h

    def group_of(khalf, place):
        even = lax.rem(side + khalf + 1, 2)
        return even * place + (1 - even) * (groups - 1 - place)

    eq = lax.rem(side + kxh + 1, 2)
    mine = group_of(kxh, cc)

    def neighbour(dz, dc):
        zt = z + dz
        good = (zt >= 0) & (zt < nz)
        zt = lax.max(lax.min(zt, nz - 1), 0)
        over = lax.rem(lax.div(zt, half) + side, 2)
        inter = lax.div(cc + 1, nc) if dc > 0 else 0
        core = 1 - lax.min(cc, 1) if dc < 0 else 0
        if dc < 0:
            good = good & ((side == 1) | (cc > 0))
        flip = lax.rem(over + inter, 2)
        tz = flip * (nz - 1 - zt) + (1 - flip) * zt
        sz, sc = (dz + 1) // 2, (dc + 1) // 2
        stay = inter + core
        alone = (over * core == 1) & good
        return dict(good=good & jnp.logical_not(alone), alone=alone, flip=flip,
                    device=owner(tz, lax.rem(kxh + flip + core, 2), cc + dc - inter + core), sz=sz, sc=sc,
                    tsz=flip * sz + (1 - flip) * (1 - sz), tsc=stay * sc + (1 - stay) * (1 - sc))

    dirs = [(dz, dc) for dz in (-1, 0, 1) for dc in (-1, 0, 1) if dz or dc]
    near = {d: neighbour(*d) for d in dirs}

    def load(m):
        at = pl.ds(m * g, g)
        return pltpu.make_async_copy(measured_hbm.at[:, :, at], measured.at[:, :, at], in_sem.at[m])

    load_kernel = pltpu.make_async_copy(kernel_hbm, kernel, in_sem.at[groups])
    load_mask = pltpu.make_async_copy(mask_hbm, mask, in_sem.at[groups + 1])

    def step_group(i):
        m = group_of(h, lax.rem(i, nc))
        return jnp.where(i < nc, groups - 1 - m, m)

    load_mask.start()
    load_kernel.start()
    for i in range(groups):
        load(step_group(i)).start()

    def home_same(cx):
        return {"kz": z, "coil": cx, "kx": kxh}

    def home_far(cx):
        return {"kz": far, "coil": cx, "kx": 1 - kxh}

    def is_self(place):
        return stays & (cc == place)

    barrier = pltpu.get_barrier_semaphore()

    def greet(device):
        pl.semaphore_signal(barrier, inc=1, device_id=device, device_id_type=MESH)

    for i in range(nc):
        greet(owner(far, 1 - h, i))
        greet(home_far(i))

        @pl.when(jnp.logical_not(is_self(i)))
        def _():
            greet(owner(z, h, i))

        @pl.when(jnp.logical_not(stays & (c == i)))
        def _():
            greet(home_same(i))

    for d in range(1, nc):
        greet({"coil": lax.rem(c + d, nc)})
    greet({"kx": 1 - h})
    count = 2 * nc + 2 * (nc - stays.astype(jnp.int32)) + nc
    for d in dirs:
        @pl.when(near[d]["good"])
        def _():
            greet(near[d]["device"])
        count = count + near[d]["good"].astype(jnp.int32)

    def remote(src, dst, send, recv, device):
        return pltpu.make_async_remote_copy(
            src_ref=src, dst_ref=dst, send_sem=send, recv_sem=recv, device_id=device, device_id_type=MESH)

    def same_copy(i, n):
        k = pl.ds(n * CHUNK, CHUNK)
        return remote(hd.at[group_of(h, i), k], rb.at[k, :, 0, c], s_send.at[i, n], s_recv.at[c, n], owner(z, h, i))

    def same_land(cx, n):
        k = pl.ds(n * CHUNK, CHUNK)
        return remote(rb.at[k, :, 0, cx], rb.at[k, :, 0, cx], s_send.at[cx, n], s_recv.at[cx, n], home_same(cx))

    def far_copy(i, n):
        k = pl.ds(planes - (n + 1) * CHUNK, CHUNK)
        return remote(hd.at[groups - 1 - group_of(h, i), k], rb.at[k, :, 1, c], v_send.at[i, n], v_recv.at[c, n], owner(far, 1 - h, i))

    def far_land(cx, n):
        k = pl.ds(planes - (n + 1) * CHUNK, CHUNK)
        return remote(rb.at[k, :, 1, cx], rb.at[k, :, 1, cx], v_send.at[cx, n], v_recv.at[cx, n], home_far(cx))

    def kernel_copy(d):
        return remote(kb.at[c, h], kb.at[c, h], k_send.at[d], k_recv.at[d], {"coil": lax.rem(c + d, nc)})

    def kernel_land(d):
        cx = lax.rem(c + nc - d, nc)
        return remote(kb.at[cx, h], kb.at[cx, h], k_send.at[d], k_recv.at[d], {"coil": cx})

    def kernel_pass(d):
        cx = lax.rem(c + nc - d, nc)
        return remote(kb.at[cx, h], kb.at[cx, h], f_send.at[d], f_recv.at[d], {"kx": 1 - h})

    def kernel_last(d):
        cx = lax.rem(c + nc - d, nc)
        return remote(kb.at[cx, 1 - h], kb.at[cx, 1 - h], f_send.at[d], f_recv.at[d], {"kx": 1 - h})

    mask_self = is_self(c)
    mask_same = remote(hm.at[group_of(h, c)], mb.at[0], m_send.at[0], m_recv.at[0], owner(z, h, c))
    mask_far = remote(hm.at[groups - 1 - group_of(h, c)], mb.at[1], m_send.at[1], m_recv.at[1], owner(far, 1 - h, c))
    mask_same_land = remote(mb.at[0], mb.at[0], m_send.at[0], m_recv.at[0], home_same(cc))
    mask_far_land = remote(mb.at[1], mb.at[1], m_send.at[1], m_recv.at[1], home_far(cc))

    hd_rows = hd.reshape(groups * planes * 2 * coils, lanes)
    fr_rows = fr.reshape(groups * planes * 2 * coils, lanes)

    def pack(m):
        keep = jnp.concatenate([mask[m * g + i] for i in range(g)], 1) == 1
        hm[m] = jnp.where(keep, 1.0, 0.0)

        def one(coil, _):
            for ri in range(2):
                value = jnp.concatenate([measured[ri, coil, m * g + i] for i in range(g)], 1)
                hd_rows[pl.ds(m * planes * 2 * coils + ri * coils + coil, planes, stride=2 * coils), :] = jnp.where(keep, value, 0.0)
            return 0

        lax.fori_loop(0, coils, one, 0, unroll=4)

    load_kernel.wait()

    def fill(t, _):
        both = jnp.concatenate([kernel[t, 0], kernel[t, 1]], 1)
        for i in range(2):
            kb[c, i, t] = both[i * (coils // 2):(i + 1) * (coils // 2)]
        return 0

    lax.fori_loop(0, TAPS, fill, 0)
    load_mask.wait()

    def pack_all(i, _):
        m = step_group(i)
        load(m).wait()
        pack(m)

        @pl.when(i == nc - 1)
        def _():
            pl.semaphore_wait(barrier, count)
            for d in range(1, nc):
                kernel_copy(d).start()
            mask_far.start()

            def launch(i, _):
                far_copy(lax.rem(i, nc), lax.div(i, nc)).start()
                return 0

            lax.fori_loop(0, parts * nc, launch, 0)

        @pl.when((i >= nc) & jnp.logical_not(is_self(i - nc)))
        def _():
            def launch(n, _):
                same_copy(i - nc, n).start()
                return 0

            lax.fori_loop(0, parts, launch, 0)

        return 0

    lax.fori_loop(0, groups, pack_all, 0)

    @pl.when(jnp.logical_not(mask_self))
    def _():
        mask_same.start()

    @pl.when(mask_self)
    def _():
        mb[0] = hm[mine]

    @pl.when(stays)
    def _():
        rb[:, :, 0, c] = hd[mine]

    for step in range(ITERS):
        for b in range(3):
            for k in (0, planes + 1):
                xb[step, b, k] = jnp.zeros(xb.shape[3:], BF16)
            for r in (0, g + 1):
                xb[step, b, :, r] = jnp.zeros((planes + 2, row, wide), BF16)

    for step in range(ITERS):
        for sz in range(2):
            @pl.when(jnp.logical_not(near[(2 * sz - 1, 0)]["good"]))
            def _():
                hz[step, sz] = jnp.zeros(hz.shape[2:], F32)
            for sc in range(2):
                @pl.when(jnp.logical_not(near[(2 * sz - 1, 2 * sc - 1)]["good"]))
                def _():
                    hq[step, sz, sc] = jnp.zeros(hq.shape[3:], F32)
        @pl.when(jnp.logical_not(near[(0, -1)]["good"]))
        def _():
            hg[step, 0] = jnp.zeros(hg.shape[2:], F32)

    for d in range(1, nc):
        kernel_land(d).wait_recv()
        kernel_pass(d).start()
    for d in range(1, nc):
        kernel_last(d).wait_recv()
    lane = lax.broadcasted_iota(jnp.int32, (1, chans), 1)
    first = lax.rem(lax.div(lane, band), 2) == 0
    upper = lane >= 2 * band

    def swap(x):
        return jnp.where(first, pltpu.roll(x, chans - band, 1), pltpu.roll(x, band, 1))

    def sign(s):
        return jnp.where(upper, jnp.where(first, s, -s), 1.0)

    def taken(t):
        return jnp.concatenate([kb[i, j, t] for i in range(nc) for j in range(2)], 0)

    def weights(t, _):
        plain = taken(t)
        turned = swap(taken(TAPS - 1 - t))
        rows = (plain * sign(-1.0), turned * sign(1.0),
                pltpu.roll(plain, 2 * band, 1) * sign(1.0), pltpu.roll(turned, 2 * band, 1) * sign(-1.0))
        for n, value in enumerate(rows):
            hi, lo = split(value)
            w[t, n * band:(n + 1) * band, :] = jnp.concatenate([hi, hi], 1)
            w[t, chans + n * band:chans + (n + 1) * band, :] = jnp.concatenate([lo, jnp.zeros_like(lo)], 1)
        return 0

    lax.fori_loop(0, TAPS, weights, 0)

    turn = reversal(lanes)
    eye = (lax.broadcasted_iota(jnp.int32, (lanes, lanes), 0) == lax.broadcasted_iota(jnp.int32, (lanes, lanes), 1))
    both = jnp.concatenate([jnp.where(eye, 1.0, 0.0).astype(BF16), turn], 1)
    def put(step, x, k, r, n, m):
        rows = n * m * row
        j = lax.rem(lax.broadcasted_iota(jnp.int32, (rows, 1), 0), row)
        for b in range(3):
            y = x
            if b == 0:
                y = jnp.where(j > 0, pltpu.roll(x, 1, 0), 0.0)
            if b == 2:
                y = jnp.where(j < row - 1, pltpu.roll(x, rows - 1, 0), 0.0)
            hi, lo = split(y)
            xb[step, b, pl.ds(k, n), pl.ds(r, m)] = jnp.concatenate([hi, lo], 1).reshape(n, m, row, wide)

    def transpose_in(k):
        kv = planes - 1 - k
        xs, xv = rb[k, :, 0].reshape(2, band, lanes), rb[kv, :, 1].reshape(2, band, lanes)
        none = jnp.zeros((band, lanes), F32)
        ms = jnp.broadcast_to(mb[0, pl.ds(k, 1)], (band, lanes))
        mv = jnp.broadcast_to(mb[1, pl.ds(kv, 1)], (band, lanes))

        def beside(s0, v0, s1, v1):
            return jnp.concatenate([jnp.concatenate(pair, 1) for pair in ((s0, none), (none, v0), (s1, none), (none, v1))], 0)

        hi, lo = split(beside(xs[0], xv[0], xs[1], xv[1]))
        mk = beside(ms, mv, ms, mv).astype(BF16)
        t = lax.dot_general(both, jnp.concatenate([hi, lo, mk], 0), NT, preferred_element_type=F32)
        x = t[:, :chans] + t[:, chans:2 * chans]
        mt[k] = t[:, 2 * chans:]
        st[0, k] = x.reshape(g, row, chans)
        put(0, x, k + 1, 1, 1, g)

    def edge(sc, inner):
        up = eq * sc + (1 - eq) * (1 - sc)
        return up * (g - 1) if inner else up * (g + 1)

    def plane_copy(step, dz):
        v = near[(dz, 0)]
        return remote(st.at[step, planes - 1 if dz > 0 else 0], hz.at[step, v["tsz"]],
                      hz_send.at[step, v["sz"]], hz_recv.at[step, v["tsz"]], v["device"])

    def row_copy(step, dc, n):
        v = near[(0, dc)]
        k = pl.ds(n * CHUNK, CHUNK)
        return remote(st.at[step, k, edge(v["sc"], True)], hg.at[step, v["tsc"], k],
                      hg_send.at[step, v["sc"], n], hg_recv.at[step, v["tsc"], n], v["device"])

    def corner_copy(step, dz, dc):
        v = near[(dz, dc)]
        return remote(st.at[step, planes - 1 if dz > 0 else 0, edge(v["sc"], True)], hq.at[step, v["tsz"], v["tsc"]],
                      hq_send.at[step, v["sz"], v["sc"]], hq_recv.at[step, v["tsz"], v["tsc"]], v["device"])

    def start_halo(step, n):
        for dc in (1, -1):
            @pl.when(near[(0, dc)]["good"])
            def _():
                row_copy(step, dc, n).start()
        for dz in (-1, 1):
            @pl.when(n == (parts - 1 if dz > 0 else 0))
            def _():
                @pl.when(near[(dz, 0)]["good"])
                def _():
                    plane_copy(step, dz).start()
                for dc in (1, -1):
                    @pl.when(near[(dz, dc)]["good"])
                    def _():
                        corner_copy(step, dz, dc).start()
                v = near[(dz, -1)]

                @pl.when(v["alone"])
                def _():
                    hq[step, v["sz"], v["sc"]] = st[step, planes - 1 if dz > 0 else 0, edge(v["sc"], True)]

    def flipped(x, rows):
        hi, lo = split(x)
        y = jnp.dot(reversal(rows), jnp.concatenate([hi, lo], 1), preferred_element_type=F32)
        return swap(y[:, :chans] + y[:, chans:])

    def place_halo(step, d, buf, n, m):
        rows = n * m * row
        x = buf[...].reshape(rows, chans)
        x = jnp.where(near[d]["flip"] == 1, flipped(x, rows), x)
        k = 1 if d[0] == 0 else (planes + 1 if d[0] > 0 else 0)
        r = 1 if d[1] == 0 else edge(near[d]["sc"], False)
        put(step, x, k, r, n, m)

    def product(xs, ws):
        p = lax.dot_general(jnp.concatenate(xs, 1), jnp.concatenate(ws, 1), NT, preferred_element_type=F32)
        return p[:, :chans] + p[:, chans:]

    def inner(step, n):
        p = product([xb[step, (t // 3) % 3, pl.ds(n * CHUNK + t % 3, CHUNK), pl.ds(t // 9, g)].reshape(CHUNK * lanes, wide)
                     for t in range(TAPS)], [w[t] for t in range(TAPS)])
        acc[pl.ds(n * CHUNK, CHUNK)] = p.reshape(CHUNK, g, row, chans)

    def outer(step):
        for dz in (-1, 1):
            v = near[(dz, 0)]
            buf = hz.at[step, v["sz"]]

            @pl.when(v["good"])
            def _():
                remote(buf, buf, hz_send.at[step, v["sz"]], hz_recv.at[step, v["sz"]], v["device"]).wait_recv()

            place_halo(step, (dz, 0), buf, 1, g)
            at, e = (planes - 1, 2) if dz > 0 else (0, 0)
            taps = [9 * a + 3 * b + e for a in range(3) for b in range(3)]
            p = product([xb[step, (t // 3) % 3, at + e, t // 9:t // 9 + g].reshape(lanes, wide) for t in taps],
                        [w[t] for t in taps])
            acc[at] += p.reshape(g, row, chans)
        for dc in (-1, 1):
            v = near[(0, dc)]
            buf = hg.at[step, v["sc"]]

            @pl.when(v["good"])
            def _():
                for n in range(parts):
                    part = buf.at[pl.ds(n * CHUNK, CHUNK)]
                    remote(part, part, hg_send.at[step, v["sc"], n], hg_recv.at[step, v["sc"], n], v["device"]).wait_recv()

            place_halo(step, (0, dc), buf, planes, 1)
            for dz in (-1, 1):
                u = near[(dz, dc)]
                corner = hq.at[step, u["sz"], u["sc"]]

                @pl.when(u["good"])
                def _():
                    remote(corner, corner, hq_send.at[step, u["sz"], u["sc"]], hq_recv.at[step, u["sz"], u["sc"]],
                           u["device"]).wait_recv()

                place_halo(step, (dz, dc), corner, 1, 1)
        for r, a in ((0, 0), (g - 1, 2)):
            taps = [9 * a + t for t in range(9)]
            p = product([xb[step, (t // 3) % 3, t % 3:t % 3 + planes, r + a].reshape(planes * row, wide) for t in taps],
                        [w[t] for t in taps])
            acc[:, r] += p.reshape(planes, row, chans)

    mask_far_land.wait_recv()

    @pl.when(jnp.logical_not(stays & (c == cc)))
    def _():
        mask_same_land.wait_recv()

    def update(step, k):
        x = jnp.where(mt[k] > 0.5, st[0, k].reshape(lanes, chans), acc[k].reshape(lanes, chans))
        st[step, k] = x.reshape(g, row, chans)
        put(step, x, k + 1, 1, 1, g)

    def stage(step, _):
        def chunk(n, _):
            @pl.when((step == 0) & (n < parts))
            def _():
                for cx in range(nc):
                    @pl.when(jnp.logical_not(stays & (c == cx)))
                    def _():
                        same_land(cx, n).wait_recv()

                    far_land(cx, n).wait_recv()
                for i in range(CHUNK):
                    transpose_in(n * CHUNK + i)
                start_halo(step, n)

            @pl.when((step > 0) & (n == 0))
            def _():
                def renew(m, _):
                    for i in range(CHUNK):
                        update(step, m * CHUNK + i)
                    start_halo(step, m)
                    return 0

                lax.fori_loop(0, parts, renew, 0)

            @pl.when(n > 0)
            def _():
                inner(step, n - 1)

            return 0

        lax.fori_loop(0, parts + 1, chunk, 0)
        outer(step)
        return 0

    lax.fori_loop(0, ITERS, stage, 0)

    def same_back(cx, n):
        k = pl.ds(n * CHUNK, CHUNK)
        return remote(ob.at[k, :, 0, cx], fr.at[mine, k], os_send.at[cx, n], os_recv.at[cc, n], home_same(cx))

    def far_back(cx, n):
        k = pl.ds(planes - (n + 1) * CHUNK, CHUNK)
        return remote(ob.at[k, :, 1, cx], fr.at[groups - 1 - mine, k], ov_send.at[cx, n], ov_recv.at[cc, n], home_far(cx))

    turn2 = jnp.concatenate([turn, turn], 1)

    def finish(n, _):
        for i in range(CHUNK):
            k = n * CHUNK + i
            r = acc[k].reshape(lanes, chans)
            hi, lo = split(r)
            back = jnp.dot(turn2, jnp.concatenate([hi, lo], 0), preferred_element_type=F32)
            y = jnp.where(first, r, back).T.reshape(2, 2, nc, coils, lanes)
            ob[k, :, 0] = y[:, 0]
            ob[planes - 1 - k, :, 1] = y[:, 1]
        for cx in range(nc):
            far_back(cx, n).start()
        for cx in range(nc):
            @pl.when(jnp.logical_not(stays & (c == cx)))
            def _():
                same_back(cx, n).start()

        return 0

    lax.fori_loop(0, parts, finish, 0)

    @pl.when(stays)
    def _():
        fr[mine] = ob[:, :, 0, c]

    def unpack(m):
        keep = hm[m] > 0.5

        def one(coil, _):
            for ri in range(2):
                at = pl.ds(m * planes * 2 * coils + ri * coils + coil, planes, stride=2 * coils)
                value = jnp.where(keep, hd_rows[at, :], fr_rows[at, :])
                for i in range(g):
                    out[ri, coil, m * g + i] = value[:, i * row:(i + 1) * row]
            return 0

        lax.fori_loop(0, coils, one, 0, unroll=4)

    def home(i, _):
        place = lax.rem(i, nc)
        m = group_of(h, place)

        def same_home(n, _):
            k = pl.ds(n * CHUNK, CHUNK)
            remote(fr.at[m, k], fr.at[m, k], os_send.at[place, n], os_recv.at[place, n], owner(z, h, place)).wait_recv()
            return 0

        def far_home(n, _):
            k = pl.ds(planes - (n + 1) * CHUNK, CHUNK)
            there = fr.at[groups - 1 - m, k]
            remote(there, there, ov_send.at[place, n], ov_recv.at[place, n], owner(far, 1 - h, place)).wait_recv()
            return 0

        @pl.when((i < nc) & jnp.logical_not(is_self(place)))
        def _():
            lax.fori_loop(0, parts, same_home, 0)

        @pl.when(i >= nc)
        def _():
            lax.fori_loop(0, parts, far_home, 0)

        unpack(jnp.where(i < nc, m, groups - 1 - m))
        return 0

    lax.fori_loop(0, groups, home, 0)

    def sent(n, _):
        for i in range(nc):
            far_copy(i, n).wait_send()
            far_back(i, n).wait_send()

            @pl.when(jnp.logical_not(is_self(i)))
            def _():
                same_copy(i, n).wait_send()

            @pl.when(jnp.logical_not(stays & (c == i)))
            def _():
                same_back(i, n).wait_send()

        return 0

    lax.fori_loop(0, parts, sent, 0)
    for d in range(1, nc):
        kernel_copy(d).wait_send()
        kernel_pass(d).wait_send()
    mask_far.wait_send()

    @pl.when(jnp.logical_not(mask_self))
    def _():
        mask_same.wait_send()

    def passed(step, _):
        for d in dirs:
            @pl.when(near[d]["good"])
            def _():
                if d[1] == 0:
                    plane_copy(step, d[0]).wait_send()
                elif d[0] == 0:
                    for n in range(parts):
                        row_copy(step, d[1], n).wait_send()
                else:
                    corner_copy(step, *d).wait_send()

        return 0

    lax.fori_loop(0, ITERS, passed, 0)


def on_device(sizes, measured, mask, kernel):
    nz, nc = sizes
    _, coils, depth_x, planes, row = measured.shape
    groups = 2 * nc
    g = depth_x // groups
    lanes = g * row
    chans = 4 * nc * coils
    parts = planes // CHUNK
    vmem = pl.BlockSpec(memory_space=pltpu.VMEM)
    dma = pltpu.SemaphoreType.DMA
    return pl.pallas_call(
        functools.partial(body, sizes),
        out_shape=jax.ShapeDtypeStruct(measured.shape, F32),
        in_specs=[pl.BlockSpec(memory_space=pl.ANY)] * 3,
        out_specs=vmem,
        scratch_shapes=[
            pltpu.VMEM(measured.shape, F32),
            pltpu.VMEM(mask.shape, jnp.int32),
            pltpu.VMEM(kernel.shape, F32),
            pltpu.VMEM((groups, planes, 2, coils, lanes), F32),
            pltpu.VMEM((groups, planes, lanes), F32),
            pltpu.VMEM((planes, 2, 2, nc, coils, lanes), F32),
            pltpu.VMEM((2, planes, lanes), F32),
            pltpu.VMEM((nc, 2, TAPS, coils // 2, chans), F32),
            pltpu.VMEM((TAPS, 2 * chans, 2 * chans), BF16),
            pltpu.VMEM((ITERS, planes, g, row, chans), F32),
            pltpu.VMEM((planes, lanes, chans), F32),
            pltpu.VMEM((ITERS, 3, planes + 2, g + 2, row, 2 * chans), BF16),
            pltpu.VMEM((ITERS, 2, g, row, chans), F32),
            pltpu.VMEM((ITERS, 2, planes, row, chans), F32),
            pltpu.VMEM((ITERS, 2, 2, row, chans), F32),
            pltpu.VMEM((planes, g, row, chans), F32),
            pltpu.VMEM((planes, 2, 2, nc, coils, lanes), F32),
            pltpu.VMEM((groups, planes, 2, coils, lanes), F32),
            dma((groups + 2,)),
            dma((nc, parts)), dma((nc, parts)), dma((nc, parts)), dma((nc, parts)),
            dma((nc,)), dma((nc,)), dma((nc,)), dma((nc,)), dma((2,)), dma((2,)),
            dma((ITERS, 2)), dma((ITERS, 2)), dma((ITERS, 2, parts)), dma((ITERS, 2, parts)),
            dma((ITERS, 2, 2)), dma((ITERS, 2, 2)),
            dma((nc, parts)), dma((nc, parts)), dma((nc, parts)), dma((nc, parts)),
        ],
        compiler_params=pltpu.CompilerParams(collective_id=0, has_side_effects=True, vmem_limit_bytes=56 << 20),
    )(measured, mask, kernel)


def solution(mesh):
    placed = (
        P(None, ("grp", "coil"), "kx", "kz", None),
        P(("grp", "kx"), "kz", None),
        P(None, None, "coil", None),
    )
    return jax.shard_map(
        functools.partial(on_device, (mesh.shape["kz"], mesh.shape["coil"])),
        mesh=mesh,
        in_specs=placed,
        out_specs=P(None, ("grp", "coil"), "kx", "kz", None),
        check_vma=False,
    )
```

time: 62.2 us -> 54.8 us (0.88)
  Pallas kernels: 58.9 us -> 51.2 us
    pallas_call x1, Pallas kernels: 58.9 us -> 51.2 us  [on_device(): pl.pallas_call(functools.partial(body, sizes), out_shape=jax.ShapeDtypeSt...]
where the time goes in v2:
time: 54.8 us; the launch traced here: 54.4 us
  Pallas kernels  51.2 us (93%)
  local copies, waits for them, and re-layouts  3.14 us (6%)
    pallas_call x1, Pallas kernels, on_device(): pl.pallas_call(functools.partial(body, sizes), out_shape=jax.ShapeDtypeSt...  51.2 us
    unnamed x1, local copies, waits for them, and re-layouts  3.14 us

profile of v2, /device:TPU:9, one launch (start us, length us, event | category | flops | bytes accessed | tf_op | source)
XLA Modules:
  0.0 54.4 jit_solution(3693636739712658194)
XLA Ops:
  0.0 51.2 %shard_map.37 = f32[2,16,16,8,32]{4,3,2,1,0:T(8,128)} custom-call(f32[2,16,16,8,32]{4,3,2,1,0:T(8,128)} %measured_hbm.1, s32[16,8,32]{2,1,0:T(8,128)} %mask_hbm.1, f32[27,2,16,64]{3,2,1,0:T(8,128)} %kernel_hbm.1), custom_call_target="tpu_custom_call" | custom-call | tf_op jit(solution)/shard_map/pallas_call | solution.py:606
  51.2 3.1 %copy.5 = f32[2,16,16,8,32]{4,3,2,1,0:T(8,128)} copy(f32[2,16,16,8,32]{4,3,2,1,0:T(8,128)} %shard_map.37) | data formatting | bytes 1048576

commit v3 on v2

--- a/solution.py
+++ b/solution.py
@@ -10,6 +10,7 @@
 ITERS = 2
 TAPS = 27
 CHUNK = 2
+VLIM = 40
 MESH = pl.DeviceIdType.MESH
 F32, BF16 = jnp.float32, jnp.bfloat16
 NT = (((1,), (1,)), ((), ()))
@@ -172,73 +173,55 @@
     mask_same_land = remote(mb.at[0], mb.at[0], m_send.at[0], m_recv.at[0], home_same(cc))
     mask_far_land = remote(mb.at[1], mb.at[1], m_send.at[1], m_recv.at[1], home_far(cc))
 
+    def visit(i):
+        return jnp.where(i == 0, 0, jnp.where(i == 1, parts - 1, i - 1))
+
     hd_rows = hd.reshape(groups * planes * 2 * coils, lanes)
-    fr_rows = fr.reshape(groups * planes * 2 * coils, lanes)
 
     def pack(m):
         keep = jnp.concatenate([mask[m * g + i] for i in range(g)], 1) == 1
         hm[m] = jnp.where(keep, 1.0, 0.0)
 
-        def one(coil, _):
-            for ri in range(2):
-                value = jnp.concatenate([measured[ri, coil, m * g + i] for i in range(g)], 1)
-                hd_rows[pl.ds(m * planes * 2 * coils + ri * coils + coil, planes, stride=2 * coils), :] = jnp.where(keep, value, 0.0)
+        for ri in range(2):
+            value = jnp.concatenate([measured[ri, :, m * g + i] for i in range(g)], 2)
+            value = jnp.where(keep, value, 0.0)
+            for coil in range(coils):
+                hd_rows[pl.ds(m * planes * 2 * coils + ri * coils + coil, planes, stride=2 * coils), :] = value[coil]
+
+    load_kernel.wait()
+
+    joined = jnp.concatenate([kernel[:, 0], kernel[:, 1]], 2)
+    for i in range(2):
+        kb[c, i] = joined[:, i * (coils // 2):(i + 1) * (coils // 2)]
+
+    lane = lax.broadcasted_iota(jnp.int32, (1, chans), 1)
+    first = lax.rem(lax.div(lane, band), 2) == 0
+    upper = lane >= 2 * band
+
+    def swap(x):
+        return jnp.where(first, pltpu.roll(x, chans - band, 1), pltpu.roll(x, band, 1))
+
+    def sign(s):
+        return jnp.where(upper, jnp.where(first, s, -s), 1.0)
+
+    def weights(cx):
+        def some(n, _):
+            plain = jnp.concatenate([kb[cx, j, pl.ds(9 * n, 9)] for j in range(2)], 1).reshape(9 * coils, chans)
+            turned = swap(plain)
+            rows = (plain * sign(-1.0), turned * sign(1.0),
+                    pltpu.roll(plain, 2 * band, 1) * sign(1.0), pltpu.roll(turned, 2 * band, 1) * sign(-1.0))
+            for i, value in enumerate(rows):
+                hi, lo = split(value)
+                at = pl.multiple_of(i * band + cx * coils, coils)
+                hi = jnp.concatenate([hi, hi], 1)
+                lo = jnp.concatenate([lo, jnp.zeros_like(lo)], 1)
+                for t in range(9):
+                    tap = TAPS - 1 - (9 * n + t) if i % 2 else 9 * n + t
+                    w[tap, pl.ds(at, coils), :] = hi[t * coils:(t + 1) * coils]
+                    w[tap, pl.ds(chans + at, coils), :] = lo[t * coils:(t + 1) * coils]
             return 0
 
-        lax.fori_loop(0, coils, one, 0, unroll=4)
-
-    load_kernel.wait()
-
-    def fill(t, _):
-        both = jnp.concatenate([kernel[t, 0], kernel[t, 1]], 1)
-        for i in range(2):
-            kb[c, i, t] = both[i * (coils // 2):(i + 1) * (coils // 2)]
-        return 0
-
-    lax.fori_loop(0, TAPS, fill, 0)
-    load_mask.wait()
-
-    def pack_all(i, _):
-        m = step_group(i)
-        load(m).wait()
-        pack(m)
-
-        @pl.when(i == nc - 1)
-        def _():
-            pl.semaphore_wait(barrier, count)
-            for d in range(1, nc):
-                kernel_copy(d).start()
-            mask_far.start()
-
-            def launch(i, _):
-                far_copy(lax.rem(i, nc), lax.div(i, nc)).start()
-                return 0
-
-            lax.fori_loop(0, parts * nc, launch, 0)
-
-        @pl.when((i >= nc) & jnp.logical_not(is_self(i - nc)))
-        def _():
-            def launch(n, _):
-                same_copy(i - nc, n).start()
-                return 0
-
-            lax.fori_loop(0, parts, launch, 0)
-
-        return 0
-
-    lax.fori_loop(0, groups, pack_all, 0)
-
-    @pl.when(jnp.logical_not(mask_self))
-    def _():
-        mask_same.start()
-
-    @pl.when(mask_self)
-    def _():
-        mb[0] = hm[mine]
-
-    @pl.when(stays)
-    def _():
-        rb[:, :, 0, c] = hd[mine]
+        lax.fori_loop(0, TAPS // 9, some, 0)
 
     for step in range(ITERS):
         for b in range(3):
@@ -260,36 +243,57 @@
         def _():
             hg[step, 0] = jnp.zeros(hg.shape[2:], F32)
 
+    load_mask.wait()
+
+    def pack_all(i, _):
+        m = step_group(i)
+        load(m).wait()
+        pack(m)
+
+        @pl.when(i == nc - 1)
+        def _():
+            pl.semaphore_wait(barrier, count)
+            for d in range(1, nc):
+                kernel_copy(d).start()
+            mask_far.start()
+
+            def launch(i, _):
+                far_copy(lax.rem(i, nc), visit(lax.div(i, nc))).start()
+                return 0
+
+            lax.fori_loop(0, parts * nc, launch, 0)
+
+        @pl.when((i >= nc) & jnp.logical_not(is_self(i - nc)))
+        def _():
+            def launch(n, _):
+                same_copy(i - nc, visit(n)).start()
+                return 0
+
+            lax.fori_loop(0, parts, launch, 0)
+
+        return 0
+
+    lax.fori_loop(0, groups, pack_all, 0)
+
+    @pl.when(jnp.logical_not(mask_self))
+    def _():
+        mask_same.start()
+
+    @pl.when(mask_self)
+    def _():
+        mb[0] = hm[mine]
+
+    @pl.when(stays)
+    def _():
+        rb[:, :, 0, c] = hd[mine]
+
+    weights(c)
     for d in range(1, nc):
         kernel_land(d).wait_recv()
         kernel_pass(d).start()
     for d in range(1, nc):
         kernel_last(d).wait_recv()
-    lane = lax.broadcasted_iota(jnp.int32, (1, chans), 1)
-    first = lax.rem(lax.div(lane, band), 2) == 0
-    upper = lane >= 2 * band
-
-    def swap(x):
-        return jnp.where(first, pltpu.roll(x, chans - band, 1), pltpu.roll(x, band, 1))
-
-    def sign(s):
-        return jnp.where(upper, jnp.where(first, s, -s), 1.0)
-
-    def taken(t):
-        return jnp.concatenate([kb[i, j, t] for i in range(nc) for j in range(2)], 0)
-
-    def weights(t, _):
-        plain = taken(t)
-        turned = swap(taken(TAPS - 1 - t))
-        rows = (plain * sign(-1.0), turned * sign(1.0),
-                pltpu.roll(plain, 2 * band, 1) * sign(1.0), pltpu.roll(turned, 2 * band, 1) * sign(-1.0))
-        for n, value in enumerate(rows):
-            hi, lo = split(value)
-            w[t, n * band:(n + 1) * band, :] = jnp.concatenate([hi, hi], 1)
-            w[t, chans + n * band:chans + (n + 1) * band, :] = jnp.concatenate([lo, jnp.zeros_like(lo)], 1)
-        return 0
-
-    lax.fori_loop(0, TAPS, weights, 0)
+        weights(lax.rem(c + d, nc))
 
     turn = reversal(lanes)
     eye = (lax.broadcasted_iota(jnp.int32, (lanes, lanes), 0) == lax.broadcasted_iota(jnp.int32, (lanes, lanes), 1))
@@ -297,32 +301,31 @@
     def put(step, x, k, r, n, m):
         rows = n * m * row
         j = lax.rem(lax.broadcasted_iota(jnp.int32, (rows, 1), 0), row)
+        shifted = (jnp.where(j > 0, pltpu.roll(x, 1, 0), 0.0), x, jnp.where(j < row - 1, pltpu.roll(x, rows - 1, 0), 0.0))
+        shifted = [jnp.concatenate(split(y), 1).reshape(n, m, row, wide) for y in shifted]
         for b in range(3):
-            y = x
-            if b == 0:
-                y = jnp.where(j > 0, pltpu.roll(x, 1, 0), 0.0)
-            if b == 2:
-                y = jnp.where(j < row - 1, pltpu.roll(x, rows - 1, 0), 0.0)
-            hi, lo = split(y)
-            xb[step, b, pl.ds(k, n), pl.ds(r, m)] = jnp.concatenate([hi, lo], 1).reshape(n, m, row, wide)
-
-    def transpose_in(k):
-        kv = planes - 1 - k
-        xs, xv = rb[k, :, 0].reshape(2, band, lanes), rb[kv, :, 1].reshape(2, band, lanes)
+            xb[step, b, pl.ds(k, n), pl.ds(r, m)] = shifted[b]
+
+    def transpose_in(k0):
         none = jnp.zeros((band, lanes), F32)
-        ms = jnp.broadcast_to(mb[0, pl.ds(k, 1)], (band, lanes))
-        mv = jnp.broadcast_to(mb[1, pl.ds(kv, 1)], (band, lanes))
 
         def beside(s0, v0, s1, v1):
             return jnp.concatenate([jnp.concatenate(pair, 1) for pair in ((s0, none), (none, v0), (s1, none), (none, v1))], 0)
 
-        hi, lo = split(beside(xs[0], xv[0], xs[1], xv[1]))
-        mk = beside(ms, mv, ms, mv).astype(BF16)
-        t = lax.dot_general(both, jnp.concatenate([hi, lo, mk], 0), NT, preferred_element_type=F32)
-        x = t[:, :chans] + t[:, chans:2 * chans]
-        mt[k] = t[:, 2 * chans:]
-        st[0, k] = x.reshape(g, row, chans)
-        put(0, x, k + 1, 1, 1, g)
+        operands = []
+        for k in range(CHUNK):
+            k = k0 + k
+            kv = planes - 1 - k
+            xs, xv = rb[k, :, 0].reshape(2, band, lanes), rb[kv, :, 1].reshape(2, band, lanes)
+            ms = jnp.broadcast_to(mb[0, pl.ds(k, 1)], (band, lanes))
+            mv = jnp.broadcast_to(mb[1, pl.ds(kv, 1)], (band, lanes))
+            operands += [*split(beside(xs[0], xv[0], xs[1], xv[1])), beside(ms, mv, ms, mv).astype(BF16)]
+        t = lax.dot_general(both, jnp.concatenate(operands, 0), NT, preferred_element_type=F32)
+        t = [t[:, i * chans:(i + 1) * chans] for i in range(3 * CHUNK)]
+        x = jnp.concatenate([t[3 * i] + t[3 * i + 1] for i in range(CHUNK)], 0)
+        mt[pl.ds(k0, CHUNK)] = jnp.concatenate([t[3 * i + 2] for i in range(CHUNK)], 0).reshape(CHUNK, lanes, chans)
+        st[0, pl.ds(k0, CHUNK)] = x.reshape(CHUNK, g, row, chans)
+        put(0, x, k0 + 1, 1, CHUNK, g)
 
     def edge(sc, inner):
         up = eq * sc + (1 - eq) * (1 - sc)
@@ -382,12 +385,14 @@
         p = lax.dot_general(jnp.concatenate(xs, 1), jnp.concatenate(ws, 1), NT, preferred_element_type=F32)
         return p[:, :chans] + p[:, chans:]
 
-    def inner(step, n):
-        p = product([xb[step, (t // 3) % 3, pl.ds(n * CHUNK + t % 3, CHUNK), pl.ds(t // 9, g)].reshape(CHUNK * lanes, wide)
-                     for t in range(TAPS)], [w[t] for t in range(TAPS)])
-        acc[pl.ds(n * CHUNK, CHUNK)] = p.reshape(CHUNK, g, row, chans)
-
-    def outer(step):
+    def convolve(step, n):
+        return product([xb[step, (t // 3) % 3, pl.ds(n * CHUNK + t % 3, CHUNK), pl.ds(t // 9, g)].reshape(CHUNK * lanes, wide)
+                        for t in range(TAPS)], [w[t] for t in range(TAPS)])
+
+    def inner(n):
+        acc[pl.ds(n * CHUNK, CHUNK)] = convolve(0, n).reshape(CHUNK, g, row, chans)
+
+    def take_planes(step):
         for dz in (-1, 1):
             v = near[(dz, 0)]
             buf = hz.at[step, v["sz"]]
@@ -397,11 +402,8 @@
                 remote(buf, buf, hz_send.at[step, v["sz"]], hz_recv.at[step, v["sz"]], v["device"]).wait_recv()
 
             place_halo(step, (dz, 0), buf, 1, g)
-            at, e = (planes - 1, 2) if dz > 0 else (0, 0)
-            taps = [9 * a + 3 * b + e for a in range(3) for b in range(3)]
-            p = product([xb[step, (t // 3) % 3, at + e, t // 9:t // 9 + g].reshape(lanes, wide) for t in taps],
-                        [w[t] for t in taps])
-            acc[at] += p.reshape(g, row, chans)
+
+    def take_rows(step):
         for dc in (-1, 1):
             v = near[(0, dc)]
             buf = hg.at[step, v["sc"]]
@@ -423,9 +425,11 @@
                            u["device"]).wait_recv()
 
                 place_halo(step, (dz, dc), corner, 1, 1)
+
+    def add_rows():
         for r, a in ((0, 0), (g - 1, 2)):
             taps = [9 * a + t for t in range(9)]
-            p = product([xb[step, (t // 3) % 3, t % 3:t % 3 + planes, r + a].reshape(planes * row, wide) for t in taps],
+            p = product([xb[0, (t // 3) % 3, t % 3:t % 3 + planes, r + a].reshape(planes * row, wide) for t in taps],
                         [w[t] for t in taps])
             acc[:, r] += p.reshape(planes, row, chans)
 
@@ -436,45 +440,50 @@
         mask_same_land.wait_recv()
 
     def update(step, k):
-        x = jnp.where(mt[k] > 0.5, st[0, k].reshape(lanes, chans), acc[k].reshape(lanes, chans))
-        st[step, k] = x.reshape(g, row, chans)
-        put(step, x, k + 1, 1, 1, g)
-
-    def stage(step, _):
-        def chunk(n, _):
-            @pl.when((step == 0) & (n < parts))
-            def _():
-                for cx in range(nc):
-                    @pl.when(jnp.logical_not(stays & (c == cx)))
-                    def _():
-                        same_land(cx, n).wait_recv()
-
-                    far_land(cx, n).wait_recv()
-                for i in range(CHUNK):
-                    transpose_in(n * CHUNK + i)
-                start_halo(step, n)
-
-            @pl.when((step > 0) & (n == 0))
-            def _():
-                def renew(m, _):
-                    for i in range(CHUNK):
-                        update(step, m * CHUNK + i)
-                    start_halo(step, m)
-                    return 0
-
-                lax.fori_loop(0, parts, renew, 0)
-
-            @pl.when(n > 0)
-            def _():
-                inner(step, n - 1)
-
-            return 0
-
-        lax.fori_loop(0, parts + 1, chunk, 0)
-        outer(step)
-        return 0
-
-    lax.fori_loop(0, ITERS, stage, 0)
+        k = pl.ds(k, CHUNK)
+        rows = CHUNK * lanes
+        x = jnp.where(mt[k].reshape(rows, chans) > 0.5, st[0, k].reshape(rows, chans), acc[k].reshape(rows, chans))
+        st[step, k] = x.reshape(CHUNK, g, row, chans)
+        put(step, x, k.start + 1, 1, CHUNK, g)
+
+    def arrive(i, _):
+        n = visit(i)
+        for cx in range(nc):
+            @pl.when(jnp.logical_not(stays & (c == cx)))
+            def _():
+                same_land(cx, n).wait_recv()
+
+            far_land(cx, n).wait_recv()
+        transpose_in(n * CHUNK)
+        start_halo(0, n)
+
+        @pl.when(i > 2)
+        def _():
+            inner(n - 1)
+
+        return 0
+
+    lax.fori_loop(0, parts, arrive, 0)
+
+    def rest(n, _):
+        inner(n)
+        return 0
+
+    take_planes(0)
+    inner(0)
+    lax.fori_loop(parts - 2, parts, rest, 0)
+    take_rows(0)
+    add_rows()
+
+    def renew(i, _):
+        n = visit(i)
+        update(1, n * CHUNK)
+        start_halo(1, n)
+        return 0
+
+    lax.fori_loop(0, parts, renew, 0)
+    take_planes(1)
+    take_rows(1)
 
     def same_back(cx, n):
         k = pl.ds(n * CHUNK, CHUNK)
@@ -487,14 +496,14 @@
     turn2 = jnp.concatenate([turn, turn], 1)
 
     def finish(n, _):
+        result = convolve(ITERS - 1, n)
+        r = [result[i * lanes:(i + 1) * lanes] for i in range(CHUNK)]
+        back = jnp.dot(turn2, jnp.concatenate([jnp.concatenate(split(x), 0) for x in r], 1), preferred_element_type=F32)
+        y = [jnp.where(first, r[i], back[:, i * chans:(i + 1) * chans]).T.reshape(2, 2, nc, coils, lanes) for i in range(CHUNK)]
         for i in range(CHUNK):
             k = n * CHUNK + i
-            r = acc[k].reshape(lanes, chans)
-            hi, lo = split(r)
-            back = jnp.dot(turn2, jnp.concatenate([hi, lo], 0), preferred_element_type=F32)
-            y = jnp.where(first, r, back).T.reshape(2, 2, nc, coils, lanes)
-            ob[k, :, 0] = y[:, 0]
-            ob[planes - 1 - k, :, 1] = y[:, 1]
+            ob[k, :, 0] = y[i][:, 0]
+            ob[planes - 1 - k, :, 1] = y[i][:, 1]
         for cx in range(nc):
             far_back(cx, n).start()
         for cx in range(nc):
@@ -510,18 +519,9 @@
     def _():
         fr[mine] = ob[:, :, 0, c]
 
-    def unpack(m):
-        keep = hm[m] > 0.5
-
-        def one(coil, _):
-            for ri in range(2):
-                at = pl.ds(m * planes * 2 * coils + ri * coils + coil, planes, stride=2 * coils)
-                value = jnp.where(keep, hd_rows[at, :], fr_rows[at, :])
-                for i in range(g):
-                    out[ri, coil, m * g + i] = value[:, i * row:(i + 1) * row]
-            return 0
-
-        lax.fori_loop(0, coils, one, 0, unroll=4)
+    def merge(m):
+        keep = [jnp.broadcast_to(hm[m, k:k + 1], (2 * coils, lanes)).reshape(2, coils, lanes) for k in range(planes)]
+        out[m] = jnp.stack([jnp.where(keep[k] > 0.5, hd[m, k], fr[m, k]) for k in range(planes)], 0)
 
     def home(i, _):
         place = lax.rem(i, nc)
@@ -546,7 +546,7 @@
         def _():
             lax.fori_loop(0, parts, far_home, 0)
 
-        unpack(jnp.where(i < nc, m, groups - 1 - m))
+        merge(jnp.where(i < nc, m, groups - 1 - m))
         return 0
 
     lax.fori_loop(0, groups, home, 0)
@@ -591,6 +591,30 @@
         return 0
 
     lax.fori_loop(0, ITERS, passed, 0)
+
+
+def unpack(packed, out_hbm, out, sem):
+    groups, planes, _, coils, lanes = packed.shape
+    row = out.shape[4]
+    g = lanes // row
+    rows = packed.reshape(groups * planes * 2 * coils, lanes)
+
+    def store(m):
+        at = pl.ds(m * g, g)
+        return pltpu.make_async_copy(out.at[:, :, at], out_hbm.at[:, :, at], sem.at[m])
+
+    def group(m, _):
+        for ri in range(2):
+            value = jnp.stack([rows[pl.ds(m * planes * 2 * coils + ri * coils + coil, planes, stride=2 * coils), :]
+                               for coil in range(coils)], 0)
+            for i in range(g):
+                out[ri, :, m * g + i] = value[:, :, i * row:(i + 1) * row]
+        store(m).start()
+        return 0
+
+    lax.fori_loop(0, groups, group, 0)
+    for m in range(groups):
+        store(m).wait()
 
 
 def on_device(sizes, measured, mask, kernel):
@@ -603,10 +627,10 @@
     parts = planes // CHUNK
     vmem = pl.BlockSpec(memory_space=pltpu.VMEM)
     dma = pltpu.SemaphoreType.DMA
-    return pl.pallas_call(
+    packed = pl.pallas_call(
         functools.partial(body, sizes),
-        out_shape=jax.ShapeDtypeStruct(measured.shape, F32),
-        in_specs=[pl.BlockSpec(memory_space=pl.ANY)] * 3,
+        out_shape=jax.ShapeDtypeStruct((groups, planes, 2, coils, lanes), F32),
+        in_specs=[pl.BlockSpec(memory_space=pltpu.HBM)] * 3,
         out_specs=vmem,
         scratch_shapes=[
             pltpu.VMEM(measured.shape, F32),
@@ -634,8 +658,16 @@
             dma((ITERS, 2, 2)), dma((ITERS, 2, 2)),
             dma((nc, parts)), dma((nc, parts)), dma((nc, parts)), dma((nc, parts)),
         ],
-        compiler_params=pltpu.CompilerParams(collective_id=0, has_side_effects=True, vmem_limit_bytes=56 << 20),
-    )(measured, mask, kernel)
+        compiler_params=pltpu.CompilerParams(collective_id=0, has_side_effects=True, vmem_limit_bytes=VLIM << 20),
+    )(*(pltpu.with_memory_space_constraint(x, pltpu.HBM) for x in (measured, mask, kernel)))
+    return pl.pallas_call(
+        unpack,
+        out_shape=jax.ShapeDtypeStruct(measured.shape, F32),
+        in_specs=[vmem],
+        out_specs=pl.BlockSpec(memory_space=pl.ANY),
+        scratch_shapes=[pltpu.VMEM(measured.shape, F32), dma((groups,))],
+        compiler_params=pltpu.CompilerParams(vmem_limit_bytes=16 << 20),
+    )(packed)
 
 
 def solution(mesh):

time: 54.8 us -> 47.9 us (0.87)
  Pallas kernels: 51.2 us -> 47.7 us
  local copies, waits for them, and re-layouts: 3.14 us -> 0 us
    pallas_call x1, Pallas kernels: 51.2 us -> 46.1 us  [on_device(): pl.pallas_call(functools.partial(body, sizes), out_shape=jax.ShapeDtypeSt...]
    unnamed x1 -> x0, local copies, waits for them, and re-layouts: 3.14 us -> none
    pallas_call x0 -> x1, Pallas kernels: none -> 1.61 us  [on_device(): pl.pallas_call(unpack, out_shape=jax.ShapeDtypeStruct(measured.shape, F32...]
where the time goes in v3:
time: 47.9 us; the launch traced here: 47.8 us
  Pallas kernels  47.7 us (100%)
    pallas_call x1, Pallas kernels, on_device(): pl.pallas_call(functools.partial(body, sizes), out_shape=jax.ShapeDtypeSt...  46.1 us
    pallas_call x1, Pallas kernels, on_device(): pl.pallas_call(unpack, out_shape=jax.ShapeDtypeStruct(measured.shape, F32...  1.61 us

profile of v3, /device:TPU:9, one launch (start us, length us, event | category | flops | bytes accessed | tf_op | source)
XLA Modules:
  0.0 47.8 jit_solution(5960965654626714507)
XLA Ops:
  0.0 46.1 %shard_map.37.packed = f32[4,8,2,16,128]{4,3,2,1,0:T(8,128)S(1)} custom-call(f32[2,16,16,8,32]{4,3,2,1,0:T(8,128)} %measured_hbm.1, s32[16,8,32]{2,1,0:T(8,128)} %mask_hbm.1, f32[27,2,16,64]{3,2,1,0:T(8,128)} %kernel_hbm.1), custom_call_target="tpu_custom_call" | custom-call | tf_op jit(solution)/shard_map/pallas_call | solution.py:630
  46.1 1.6 %shard_map.38 = f32[2,16,16,8,32]{4,3,2,1,0:T(8,128)} custom-call(f32[4,8,2,16,128]{4,3,2,1,0:T(8,128)S(1)} %shard_map.37.packed), custom_call_target="tpu_custom_call" | custom-call | tf_op jit(solution)/shard_map/pallas_call | solution.py:663

commit v4 on v3

--- a/solution.py
+++ b/solution.py
@@ -34,7 +34,9 @@
     half = nz // 2
     groups = 2 * nc
     g = depth_x // groups
-    lanes = g * row
+    halves = g // 2
+    plane = g * row
+    lanes = 2 * CHUNK * row
     band = nc * coils
     chans = 4 * band
     wide = 2 * chans
@@ -136,21 +138,27 @@
         return pltpu.make_async_remote_copy(
             src_ref=src, dst_ref=dst, send_sem=send, recv_sem=recv, device_id=device, device_id_type=MESH)
 
-    def same_copy(i, n):
-        k = pl.ds(n * CHUNK, CHUNK)
-        return remote(hd.at[group_of(h, i), k], rb.at[k, :, 0, c], s_send.at[i, n], s_recv.at[c, n], owner(z, h, i))
-
-    def same_land(cx, n):
-        k = pl.ds(n * CHUNK, CHUNK)
-        return remote(rb.at[k, :, 0, cx], rb.at[k, :, 0, cx], s_send.at[cx, n], s_recv.at[cx, n], home_same(cx))
-
-    def far_copy(i, n):
-        k = pl.ds(planes - (n + 1) * CHUNK, CHUNK)
-        return remote(hd.at[groups - 1 - group_of(h, i), k], rb.at[k, :, 1, c], v_send.at[i, n], v_recv.at[c, n], owner(far, 1 - h, i))
-
-    def far_land(cx, n):
-        k = pl.ds(planes - (n + 1) * CHUNK, CHUNK)
-        return remote(rb.at[k, :, 1, cx], rb.at[k, :, 1, cx], v_send.at[cx, n], v_recv.at[cx, n], home_far(cx))
+    def slot(n, q):
+        return n * CHUNK + q
+
+    def back_slot(n, q):
+        return (parts - 1 - n) * CHUNK + q
+
+    def same_copy(i, n, q):
+        k = slot(n, q)
+        return remote(hd.at[group_of(h, i), k], rb.at[k, :, 0, c], s_send.at[i, k], s_recv.at[c, k], owner(z, h, i))
+
+    def same_land(cx, n, q):
+        k = slot(n, q)
+        return remote(rb.at[k, :, 0, cx], rb.at[k, :, 0, cx], s_send.at[cx, k], s_recv.at[cx, k], home_same(cx))
+
+    def far_copy(i, n, q):
+        k = back_slot(n, q)
+        return remote(hd.at[groups - 1 - group_of(h, i), k], rb.at[k, :, 1, c], v_send.at[i, k], v_recv.at[c, k], owner(far, 1 - h, i))
+
+    def far_land(cx, n, q):
+        k = back_slot(n, q)
+        return remote(rb.at[k, :, 1, cx], rb.at[k, :, 1, cx], v_send.at[cx, k], v_recv.at[cx, k], home_far(cx))
 
     def kernel_copy(d):
         return remote(kb.at[c, h], kb.at[c, h], k_send.at[d], k_recv.at[d], {"coil": lax.rem(c + d, nc)})
@@ -178,13 +186,21 @@
 
     hd_rows = hd.reshape(groups * planes * 2 * coils, lanes)
 
+    def weave(tile):
+        a = jnp.concatenate([tile(0), tile(g - 1)], -1)
+        axis = a.ndim - 2
+        even = jnp.concatenate([a, pltpu.roll(a, planes - 1, axis)], -1)
+        if halves == 1:
+            return even
+        b = jnp.concatenate([tile(1), tile(g - 2)], -1)
+        odd = jnp.concatenate([pltpu.roll(b, 1, axis), b], -1)
+        return jnp.where(lax.rem(lax.broadcasted_iota(jnp.int32, even.shape, axis), 2) == 0, even, odd)
+
     def pack(m):
-        keep = jnp.concatenate([mask[m * g + i] for i in range(g)], 1) == 1
+        keep = weave(lambda i: mask[m * g + i]) == 1
         hm[m] = jnp.where(keep, 1.0, 0.0)
-
         for ri in range(2):
-            value = jnp.concatenate([measured[ri, :, m * g + i] for i in range(g)], 2)
-            value = jnp.where(keep, value, 0.0)
+            value = jnp.where(keep, weave(lambda i: measured[ri, :, m * g + i]), 0.0)
             for coil in range(coils):
                 hd_rows[pl.ds(m * planes * 2 * coils + ri * coils + coil, planes, stride=2 * coils), :] = value[coil]
 
@@ -257,19 +273,21 @@
                 kernel_copy(d).start()
             mask_far.start()
 
-            def launch(i, _):
-                far_copy(lax.rem(i, nc), visit(lax.div(i, nc))).start()
-                return 0
-
-            lax.fori_loop(0, parts * nc, launch, 0)
+            for q in range(halves):
+                def launch(i, _):
+                    far_copy(lax.rem(i, nc), visit(lax.div(i, nc)), q).start()
+                    return 0
+
+                lax.fori_loop(0, parts * nc, launch, 0)
 
         @pl.when((i >= nc) & jnp.logical_not(is_self(i - nc)))
         def _():
-            def launch(n, _):
-                same_copy(i - nc, visit(n)).start()
-                return 0
-
-            lax.fori_loop(0, parts, launch, 0)
+            for q in range(halves):
+                def launch(n, _):
+                    same_copy(i - nc, visit(n), q).start()
+                    return 0
+
+                lax.fori_loop(0, parts, launch, 0)
 
         return 0
 
@@ -298,34 +316,38 @@
     turn = reversal(lanes)
     eye = (lax.broadcasted_iota(jnp.int32, (lanes, lanes), 0) == lax.broadcasted_iota(jnp.int32, (lanes, lanes), 1))
     both = jnp.concatenate([jnp.where(eye, 1.0, 0.0).astype(BF16), turn], 1)
-    def put(step, x, k, r, n, m):
-        rows = n * m * row
+    def put(step, x, k, n, at):
+        rows = n * len(at) * row
         j = lax.rem(lax.broadcasted_iota(jnp.int32, (rows, 1), 0), row)
         shifted = (jnp.where(j > 0, pltpu.roll(x, 1, 0), 0.0), x, jnp.where(j < row - 1, pltpu.roll(x, rows - 1, 0), 0.0))
-        shifted = [jnp.concatenate(split(y), 1).reshape(n, m, row, wide) for y in shifted]
+        shifted = [jnp.concatenate(split(y), 1).reshape(n, len(at), row, wide) for y in shifted]
         for b in range(3):
-            xb[step, b, pl.ds(k, n), pl.ds(r, m)] = shifted[b]
-
-    def transpose_in(k0):
+            for i, r in enumerate(at):
+                xb[step, b, pl.ds(k, n), r] = shifted[b][:, i]
+
+    def pair(q):
+        return q, g - 1 - q
+
+    def transpose_in(n, q):
         none = jnp.zeros((band, lanes), F32)
 
         def beside(s0, v0, s1, v1):
-            return jnp.concatenate([jnp.concatenate(pair, 1) for pair in ((s0, none), (none, v0), (s1, none), (none, v1))], 0)
-
-        operands = []
-        for k in range(CHUNK):
-            k = k0 + k
-            kv = planes - 1 - k
-            xs, xv = rb[k, :, 0].reshape(2, band, lanes), rb[kv, :, 1].reshape(2, band, lanes)
-            ms = jnp.broadcast_to(mb[0, pl.ds(k, 1)], (band, lanes))
-            mv = jnp.broadcast_to(mb[1, pl.ds(kv, 1)], (band, lanes))
-            operands += [*split(beside(xs[0], xv[0], xs[1], xv[1])), beside(ms, mv, ms, mv).astype(BF16)]
-        t = lax.dot_general(both, jnp.concatenate(operands, 0), NT, preferred_element_type=F32)
-        t = [t[:, i * chans:(i + 1) * chans] for i in range(3 * CHUNK)]
-        x = jnp.concatenate([t[3 * i] + t[3 * i + 1] for i in range(CHUNK)], 0)
-        mt[pl.ds(k0, CHUNK)] = jnp.concatenate([t[3 * i + 2] for i in range(CHUNK)], 0).reshape(CHUNK, lanes, chans)
-        st[0, pl.ds(k0, CHUNK)] = x.reshape(CHUNK, g, row, chans)
-        put(0, x, k0 + 1, 1, CHUNK, g)
+            return jnp.concatenate([jnp.concatenate(both, 1) for both in ((s0, none), (none, v0), (s1, none), (none, v1))], 0)
+
+        ks, kv = slot(n, q), back_slot(n, q)
+        xs, xv = rb[ks, :, 0].reshape(2, band, lanes), rb[kv, :, 1].reshape(2, band, lanes)
+        ms = jnp.broadcast_to(mb[0, pl.ds(ks, 1)], (band, lanes))
+        mv = jnp.broadcast_to(mb[1, pl.ds(kv, 1)], (band, lanes))
+        operand = [*split(beside(xs[0], xv[0], xs[1], xv[1])), beside(ms, mv, ms, mv).astype(BF16)]
+        t = lax.dot_general(both, jnp.concatenate(operand, 0), NT, preferred_element_type=F32)
+        x = t[:, :chans] + t[:, chans:2 * chans]
+        kept = t[:, 2 * chans:].reshape(CHUNK, 2, row, chans)
+        here = x.reshape(CHUNK, 2, row, chans)
+        k = pl.ds(n * CHUNK, CHUNK)
+        for i, r in enumerate(pair(q)):
+            mt[k, r] = kept[:, i]
+            st[0, k, r] = here[:, i]
+        put(0, x, n * CHUNK + 1, CHUNK, [r + 1 for r in pair(q)])
 
     def edge(sc, inner):
         up = eq * sc + (1 - eq) * (1 - sc)
@@ -347,7 +369,12 @@
         return remote(st.at[step, planes - 1 if dz > 0 else 0, edge(v["sc"], True)], hq.at[step, v["tsz"], v["tsc"]],
                       hq_send.at[step, v["sz"], v["sc"]], hq_recv.at[step, v["tsz"], v["tsc"]], v["device"])
 
-    def start_halo(step, n):
+    def send_plane(step, dz):
+        @pl.when(near[(dz, 0)]["good"])
+        def _():
+            plane_copy(step, dz).start()
+
+    def send_rows(step, n):
         for dc in (1, -1):
             @pl.when(near[(0, dc)]["good"])
             def _():
@@ -355,9 +382,6 @@
         for dz in (-1, 1):
             @pl.when(n == (parts - 1 if dz > 0 else 0))
             def _():
-                @pl.when(near[(dz, 0)]["good"])
-                def _():
-                    plane_copy(step, dz).start()
                 for dc in (1, -1):
                     @pl.when(near[(dz, dc)]["good"])
                     def _():
@@ -368,6 +392,12 @@
                 def _():
                     hq[step, v["sz"], v["sc"]] = st[step, planes - 1 if dz > 0 else 0, edge(v["sc"], True)]
 
+    def send_planes(step, n):
+        for dz in (-1, 1):
+            @pl.when(n == (parts - 1 if dz > 0 else 0))
+            def _():
+                send_plane(step, dz)
+
     def flipped(x, rows):
         hi, lo = split(x)
         y = jnp.dot(reversal(rows), jnp.concatenate([hi, lo], 1), preferred_element_type=F32)
@@ -378,19 +408,15 @@
         x = buf[...].reshape(rows, chans)
         x = jnp.where(near[d]["flip"] == 1, flipped(x, rows), x)
         k = 1 if d[0] == 0 else (planes + 1 if d[0] > 0 else 0)
-        r = 1 if d[1] == 0 else edge(near[d]["sc"], False)
-        put(step, x, k, r, n, m)
+        put(step, x, k, n, range(1, g + 1) if d[1] == 0 else [edge(near[d]["sc"], False)])
 
     def product(xs, ws):
         p = lax.dot_general(jnp.concatenate(xs, 1), jnp.concatenate(ws, 1), NT, preferred_element_type=F32)
         return p[:, :chans] + p[:, chans:]
 
     def convolve(step, n):
-        return product([xb[step, (t // 3) % 3, pl.ds(n * CHUNK + t % 3, CHUNK), pl.ds(t // 9, g)].reshape(CHUNK * lanes, wide)
+        return product([xb[step, (t // 3) % 3, pl.ds(n * CHUNK + t % 3, CHUNK), pl.ds(t // 9, g)].reshape(CHUNK * plane, wide)
                         for t in range(TAPS)], [w[t] for t in range(TAPS)])
-
-    def inner(n):
-        acc[pl.ds(n * CHUNK, CHUNK)] = convolve(0, n).reshape(CHUNK, g, row, chans)
 
     def take_planes(step):
         for dz in (-1, 1):
@@ -426,10 +452,10 @@
 
                 place_halo(step, (dz, dc), corner, 1, 1)
 
-    def add_rows():
+    def add_rows(step):
         for r, a in ((0, 0), (g - 1, 2)):
             taps = [9 * a + t for t in range(9)]
-            p = product([xb[0, (t // 3) % 3, t % 3:t % 3 + planes, r + a].reshape(planes * row, wide) for t in taps],
+            p = product([xb[step, (t // 3) % 3, t % 3:t % 3 + planes, r + a].reshape(planes * row, wide) for t in taps],
                         [w[t] for t in taps])
             acc[:, r] += p.reshape(planes, row, chans)
 
@@ -439,81 +465,97 @@
     def _():
         mask_same_land.wait_recv()
 
-    def update(step, k):
-        k = pl.ds(k, CHUNK)
-        rows = CHUNK * lanes
-        x = jnp.where(mt[k].reshape(rows, chans) > 0.5, st[0, k].reshape(rows, chans), acc[k].reshape(rows, chans))
-        st[step, k] = x.reshape(CHUNK, g, row, chans)
-        put(step, x, k.start + 1, 1, CHUNK, g)
-
-    def arrive(i, _):
-        n = visit(i)
+    def landed(n, q):
         for cx in range(nc):
             @pl.when(jnp.logical_not(stays & (c == cx)))
             def _():
-                same_land(cx, n).wait_recv()
-
-            far_land(cx, n).wait_recv()
-        transpose_in(n * CHUNK)
-        start_halo(0, n)
-
-        @pl.when(i > 2)
-        def _():
-            inner(n - 1)
-
-        return 0
-
-    lax.fori_loop(0, parts, arrive, 0)
-
-    def rest(n, _):
-        inner(n)
-        return 0
-
-    take_planes(0)
-    inner(0)
-    lax.fori_loop(parts - 2, parts, rest, 0)
-    take_rows(0)
-    add_rows()
-
-    def renew(i, _):
+                same_land(cx, n, q).wait_recv()
+
+            far_land(cx, n, q).wait_recv()
+
+    def arrive_edges(i, _):
         n = visit(i)
-        update(1, n * CHUNK)
-        start_halo(1, n)
-        return 0
-
-    lax.fori_loop(0, parts, renew, 0)
-    take_planes(1)
-    take_rows(1)
-
-    def same_back(cx, n):
-        k = pl.ds(n * CHUNK, CHUNK)
-        return remote(ob.at[k, :, 0, cx], fr.at[mine, k], os_send.at[cx, n], os_recv.at[cc, n], home_same(cx))
-
-    def far_back(cx, n):
-        k = pl.ds(planes - (n + 1) * CHUNK, CHUNK)
-        return remote(ob.at[k, :, 1, cx], fr.at[groups - 1 - mine, k], ov_send.at[cx, n], ov_recv.at[cc, n], home_far(cx))
+        landed(n, 0)
+        transpose_in(n, 0)
+        send_rows(0, n)
+        return 0
+
+    lax.fori_loop(0, parts, arrive_edges, 0)
+
+    def arrive_rest(i, _):
+        n = visit(i)
+        for q in range(1, halves):
+            landed(n, q)
+            transpose_in(n, q)
+        send_planes(0, n)
+        return 0
+
+    lax.fori_loop(0, parts, arrive_rest, 0)
+
+    for step in range(ITERS - 1):
+        take_rows(step)
+        take_planes(step)
+
+        def iterate(i, _):
+            n = visit(i)
+            k = pl.ds(n * CHUNK, CHUNK)
+            rows = CHUNK * plane
+            result = convolve(step, n)
+            x = jnp.where(mt[k].reshape(rows, chans) > 0.5, st[0, k].reshape(rows, chans), result)
+            st[step + 1, k] = x.reshape(CHUNK, g, row, chans)
+            put(step + 1, x, n * CHUNK + 1, CHUNK, range(1, g + 1))
+            send_rows(step + 1, n)
+            send_planes(step + 1, n)
+            return 0
+
+        lax.fori_loop(0, parts, iterate, 0)
+
+    def same_back(cx, n, q):
+        k = slot(n, q)
+        return remote(ob.at[k, :, 0, cx], fr.at[mine, k], os_send.at[cx, k], os_recv.at[cc, k], home_same(cx))
+
+    def far_back(cx, n, q):
+        k = back_slot(n, q)
+        return remote(ob.at[k, :, 1, cx], fr.at[groups - 1 - mine, k], ov_send.at[cx, k], ov_recv.at[cc, k], home_far(cx))
 
     turn2 = jnp.concatenate([turn, turn], 1)
 
-    def finish(n, _):
-        result = convolve(ITERS - 1, n)
-        r = [result[i * lanes:(i + 1) * lanes] for i in range(CHUNK)]
-        back = jnp.dot(turn2, jnp.concatenate([jnp.concatenate(split(x), 0) for x in r], 1), preferred_element_type=F32)
-        y = [jnp.where(first, r[i], back[:, i * chans:(i + 1) * chans]).T.reshape(2, 2, nc, coils, lanes) for i in range(CHUNK)]
-        for i in range(CHUNK):
-            k = n * CHUNK + i
-            ob[k, :, 0] = y[i][:, 0]
-            ob[planes - 1 - k, :, 1] = y[i][:, 1]
+    def finish(x, n, q):
+        r = jnp.stack([x[:, i] for i in pair(q)], 1).reshape(lanes, chans)
+        back = jnp.dot(turn2, jnp.concatenate(split(r), 0), preferred_element_type=F32)
+        y = jnp.where(first, r, back).T.reshape(2, 2, nc, coils, lanes)
+        ob[slot(n, q), :, 0] = y[:, 0]
+        ob[back_slot(n, q), :, 1] = y[:, 1]
         for cx in range(nc):
-            far_back(cx, n).start()
+            far_back(cx, n, q).start()
         for cx in range(nc):
             @pl.when(jnp.logical_not(stays & (c == cx)))
             def _():
-                same_back(cx, n).start()
-
-        return 0
-
-    lax.fori_loop(0, parts, finish, 0)
+                same_back(cx, n, q).start()
+
+    def ahead(i, _):
+        n = jnp.where(i < parts - 2, i + 1, jnp.where(i == parts - 2, 0, parts - 1))
+
+        @pl.when(i == parts - 2)
+        def _():
+            take_planes(ITERS - 1)
+
+        result = convolve(ITERS - 1, n).reshape(CHUNK, g, row, chans)
+        acc[pl.ds(n * CHUNK, CHUNK)] = result
+        for q in range(1, halves):
+            finish(result, n, q)
+        return 0
+
+    lax.fori_loop(0, parts, ahead, 0)
+    take_rows(ITERS - 1)
+    add_rows(ITERS - 1)
+
+    def edges(i, _):
+        n = visit(i)
+        finish(acc[pl.ds(n * CHUNK, CHUNK)], n, 0)
+        return 0
+
+    lax.fori_loop(0, parts, edges, 0)
 
     @pl.when(stays)
     def _():
@@ -528,14 +570,17 @@
         m = group_of(h, place)
 
         def same_home(n, _):
-            k = pl.ds(n * CHUNK, CHUNK)
-            remote(fr.at[m, k], fr.at[m, k], os_send.at[place, n], os_recv.at[place, n], owner(z, h, place)).wait_recv()
+            for q in range(halves):
+                there = fr.at[m, slot(n, q)]
+                k = slot(n, q)
+                remote(there, there, os_send.at[place, k], os_recv.at[place, k], owner(z, h, place)).wait_recv()
             return 0
 
         def far_home(n, _):
-            k = pl.ds(planes - (n + 1) * CHUNK, CHUNK)
-            there = fr.at[groups - 1 - m, k]
-            remote(there, there, ov_send.at[place, n], ov_recv.at[place, n], owner(far, 1 - h, place)).wait_recv()
+            for q in range(halves):
+                k = back_slot(n, q)
+                there = fr.at[groups - 1 - m, k]
+                remote(there, there, ov_send.at[place, k], ov_recv.at[place, k], owner(far, 1 - h, place)).wait_recv()
             return 0
 
         @pl.when((i < nc) & jnp.logical_not(is_self(place)))
@@ -552,17 +597,18 @@
     lax.fori_loop(0, groups, home, 0)
 
     def sent(n, _):
-        for i in range(nc):
-            far_copy(i, n).wait_send()
-            far_back(i, n).wait_send()
-
-            @pl.when(jnp.logical_not(is_self(i)))
-            def _():
-                same_copy(i, n).wait_send()
-
-            @pl.when(jnp.logical_not(stays & (c == i)))
-            def _():
-                same_back(i, n).wait_send()
+        for q in range(halves):
+            for i in range(nc):
+                far_copy(i, n, q).wait_send()
+                far_back(i, n, q).wait_send()
+
+                @pl.when(jnp.logical_not(is_self(i)))
+                def _():
+                    same_copy(i, n, q).wait_send()
+
+                @pl.when(jnp.logical_not(stays & (c == i)))
+                def _():
+                    same_back(i, n, q).wait_send()
 
         return 0
 
@@ -596,8 +642,9 @@
 def unpack(packed, out_hbm, out, sem):
     groups, planes, _, coils, lanes = packed.shape
     row = out.shape[4]
-    g = lanes // row
+    g = out.shape[2] // groups
     rows = packed.reshape(groups * planes * 2 * coils, lanes)
+    even = lax.rem(lax.broadcasted_iota(jnp.int32, (coils, planes, 2 * row), 1), 2) == 0
 
     def store(m):
         at = pl.ds(m * g, g)
@@ -607,8 +654,11 @@
         for ri in range(2):
             value = jnp.stack([rows[pl.ds(m * planes * 2 * coils + ri * coils + coil, planes, stride=2 * coils), :]
                                for coil in range(coils)], 0)
-            for i in range(g):
-                out[ri, :, m * g + i] = value[:, :, i * row:(i + 1) * row]
+            left, right = value[:, :, :2 * row], value[:, :, 2 * row:]
+            for q in range(g // 2):
+                tile = jnp.where(even, left if q == 0 else pltpu.roll(left, planes - 1, 1), right if q else pltpu.roll(right, 1, 1))
+                out[ri, :, m * g + q] = tile[:, :, :row]
+                out[ri, :, m * g + g - 1 - q] = tile[:, :, row:]
         store(m).start()
         return 0
 
@@ -622,7 +672,7 @@
     _, coils, depth_x, planes, row = measured.shape
     groups = 2 * nc
     g = depth_x // groups
-    lanes = g * row
+    lanes = 2 * CHUNK * row
     chans = 4 * nc * coils
     parts = planes // CHUNK
     vmem = pl.BlockSpec(memory_space=pltpu.VMEM)
@@ -643,7 +693,7 @@
             pltpu.VMEM((nc, 2, TAPS, coils // 2, chans), F32),
             pltpu.VMEM((TAPS, 2 * chans, 2 * chans), BF16),
             pltpu.VMEM((ITERS, planes, g, row, chans), F32),
-            pltpu.VMEM((planes, lanes, chans), F32),
+            pltpu.VMEM((planes, g, row, chans), F32),
             pltpu.VMEM((ITERS, 3, planes + 2, g + 2, row, 2 * chans), BF16),
             pltpu.VMEM((ITERS, 2, g, row, chans), F32),
             pltpu.VMEM((ITERS, 2, planes, row, chans), F32),
@@ -652,11 +702,11 @@
             pltpu.VMEM((planes, 2, 2, nc, coils, lanes), F32),
             pltpu.VMEM((groups, planes, 2, coils, lanes), F32),
             dma((groups + 2,)),
-            dma((nc, parts)), dma((nc, parts)), dma((nc, parts)), dma((nc, parts)),
+            dma((nc, planes)), dma((nc, planes)), dma((nc, planes)), dma((nc, planes)),
             dma((nc,)), dma((nc,)), dma((nc,)), dma((nc,)), dma((2,)), dma((2,)),
             dma((ITERS, 2)), dma((ITERS, 2)), dma((ITERS, 2, parts)), dma((ITERS, 2, parts)),
             dma((ITERS, 2, 2)), dma((ITERS, 2, 2)),
-            dma((nc, parts)), dma((nc, parts)), dma((nc, parts)), dma((nc, parts)),
+            dma((nc, planes)), dma((nc, planes)), dma((nc, planes)), dma((nc, planes)),
         ],
         compiler_params=pltpu.CompilerParams(collective_id=0, has_side_effects=True, vmem_limit_bytes=VLIM << 20),
     )(*(pltpu.with_memory_space_constraint(x, pltpu.HBM) for x in (measured, mask, kernel)))

time: 47.9 us -> 45.2 us (0.944); the launches traced: 47.8 us -> 44.6 us
  Pallas kernels: 47.7 us -> 44.6 us
    pallas_call x1, Pallas kernels: 46.1 us -> 42.8 us  [on_device(): pl.pallas_call(functools.partial(body, sizes), out_shape=jax.ShapeDtypeSt...]
where the time goes in v4:
time: 45.2 us; the launch traced here: 44.6 us
  Pallas kernels  44.6 us (99%)
    pallas_call x1, Pallas kernels, on_device(): pl.pallas_call(functools.partial(body, sizes), out_shape=jax.ShapeDtypeSt...  42.8 us
    pallas_call x1, Pallas kernels, on_device(): pl.pallas_call(unpack, out_shape=jax.ShapeDtypeStruct(measured.shape, F32...  1.74 us

profile of v4, /device:TPU:9, one launch (start us, length us, event | category | flops | bytes accessed | tf_op | source)
XLA Modules:
  0.0 44.6 jit_solution(5988174984227292956)
XLA Ops:
  0.0 42.8 %shard_map.37.packed = f32[4,8,2,16,128]{4,3,2,1,0:T(8,128)S(1)} custom-call(f32[2,16,16,8,32]{4,3,2,1,0:T(8,128)} %measured_hbm.1, s32[16,8,32]{2,1,0:T(8,128)} %mask_hbm.1, f32[27,2,16,64]{3,2,1,0:T(8,128)} %kernel_hbm.1), custom_call_target="tpu_custom_call" | custom-call | tf_op jit(solution)/shard_map/pallas_call | solution.py:680
  42.8 1.7 %shard_map.38 = f32[2,16,16,8,32]{4,3,2,1,0:T(8,128)} custom-call(f32[4,8,2,16,128]{4,3,2,1,0:T(8,128)S(1)} %shard_map.37.packed), custom_call_target="tpu_custom_call" | custom-call | tf_op jit(solution)/shard_map/pallas_call | solution.py:713

commit v5 on v4

--- a/solution.py
+++ b/solution.py
@@ -344,10 +344,10 @@
         kept = t[:, 2 * chans:].reshape(CHUNK, 2, row, chans)
         here = x.reshape(CHUNK, 2, row, chans)
         k = pl.ds(n * CHUNK, CHUNK)
-        for i, r in enumerate(pair(q)):
+        for i, r in enumerate((q, g - 1 - q)):
             mt[k, r] = kept[:, i]
             st[0, k, r] = here[:, i]
-        put(0, x, n * CHUNK + 1, CHUNK, [r + 1 for r in pair(q)])
+        put(0, x, n * CHUNK + 1, CHUNK, [q + 1, g - q])
 
     def edge(sc, inner):
         up = eq * sc + (1 - eq) * (1 - sc)
@@ -403,12 +403,12 @@
         y = jnp.dot(reversal(rows), jnp.concatenate([hi, lo], 1), preferred_element_type=F32)
         return swap(y[:, :chans] + y[:, chans:])
 
-    def place_halo(step, d, buf, n, m):
-        rows = n * m * row
+    def place_halo(step, flip, buf, k, n, at):
+        rows = n * len(at) * row
         x = buf[...].reshape(rows, chans)
-        x = jnp.where(near[d]["flip"] == 1, flipped(x, rows), x)
-        k = 1 if d[0] == 0 else (planes + 1 if d[0] > 0 else 0)
-        put(step, x, k, n, range(1, g + 1) if d[1] == 0 else [edge(near[d]["sc"], False)])
+        if flip is not None:
+            x = jnp.where(flip == 1, flipped(x, rows), x)
+        put(step, x, k, n, at)
 
     def product(xs, ws):
         p = lax.dot_general(jnp.concatenate(xs, 1), jnp.concatenate(ws, 1), NT, preferred_element_type=F32)
@@ -427,7 +427,9 @@
             def _():
                 remote(buf, buf, hz_send.at[step, v["sz"]], hz_recv.at[step, v["sz"]], v["device"]).wait_recv()
 
-            place_halo(step, (dz, 0), buf, 1, g)
+        for dz in (-1, 1):
+            v = near[(dz, 0)]
+            place_halo(step, v["flip"], hz.at[step, v["sz"]], v["sz"] * (planes + 1), 1, range(1, g + 1))
 
     def take_rows(step):
         for dc in (-1, 1):
@@ -436,11 +438,13 @@
 
             @pl.when(v["good"])
             def _():
-                for n in range(parts):
+                def land(n, _):
                     part = buf.at[pl.ds(n * CHUNK, CHUNK)]
                     remote(part, part, hg_send.at[step, v["sc"], n], hg_recv.at[step, v["sc"], n], v["device"]).wait_recv()
-
-            place_halo(step, (0, dc), buf, planes, 1)
+                    return 0
+
+                lax.fori_loop(0, parts, land, 0)
+
             for dz in (-1, 1):
                 u = near[(dz, dc)]
                 corner = hq.at[step, u["sz"], u["sc"]]
@@ -450,7 +454,13 @@
                     remote(corner, corner, hq_send.at[step, u["sz"], u["sc"]], hq_recv.at[step, u["sz"], u["sc"]],
                            u["device"]).wait_recv()
 
-                place_halo(step, (dz, dc), corner, 1, 1)
+        for dc in (-1, 1):
+            v = near[(0, dc)]
+            at = [edge(v["sc"], False)]
+            place_halo(step, v["flip"] if dc > 0 else None, hg.at[step, v["sc"]], 1, planes, at)
+            for dz in (-1, 1):
+                u = near[(dz, dc)]
+                place_halo(step, u["flip"], hq.at[step, u["sz"], u["sc"]], u["sz"] * (planes + 1), 1, at)
 
     def add_rows(step):
         for r, a in ((0, 0), (g - 1, 2)):
@@ -473,24 +483,22 @@
 
             far_land(cx, n, q).wait_recv()
 
-    def arrive_edges(i, _):
-        n = visit(i)
-        landed(n, 0)
-        transpose_in(n, 0)
-        send_rows(0, n)
+    def arrive(i, _):
+        n, q = visit(lax.rem(i, parts)), lax.div(i, parts)
+        landed(n, q)
+        transpose_in(n, q)
+
+        @pl.when(q == 0)
+        def _():
+            send_rows(0, n)
+
+        @pl.when(q == halves - 1)
+        def _():
+            send_planes(0, n)
+
         return 0
 
-    lax.fori_loop(0, parts, arrive_edges, 0)
-
-    def arrive_rest(i, _):
-        n = visit(i)
-        for q in range(1, halves):
-            landed(n, q)
-            transpose_in(n, q)
-        send_planes(0, n)
-        return 0
-
-    lax.fori_loop(0, parts, arrive_rest, 0)
+    lax.fori_loop(0, parts * halves, arrive, 0)
 
     for step in range(ITERS - 1):
         take_rows(step)

time: 45.2 us -> 43.8 us (0.969)
  Pallas kernels: 44.6 us -> 43.2 us
    pallas_call x1, Pallas kernels: 42.8 us -> 41.5 us  [on_device(): pl.pallas_call(functools.partial(body, sizes), out_shape=jax.ShapeDtypeSt...]
where the time goes in v5:
time: 43.8 us; the launch traced here: 43.2 us
  Pallas kernels  43.2 us (99%)
    pallas_call x1, Pallas kernels, on_device(): pl.pallas_call(functools.partial(body, sizes), out_shape=jax.ShapeDtypeSt...  41.5 us
    pallas_call x1, Pallas kernels, on_device(): pl.pallas_call(unpack, out_shape=jax.ShapeDtypeStruct(measured.shape, F32...  1.74 us

profile of v5, /device:TPU:9, one launch (start us, length us, event | category | flops | bytes accessed | tf_op | source)
XLA Modules:
  0.0 43.2 jit_solution(2098602596315696891)
XLA Ops:
  0.0 41.5 %shard_map.37.packed = f32[4,8,2,16,128]{4,3,2,1,0:T(8,128)S(1)} custom-call(f32[2,16,16,8,32]{4,3,2,1,0:T(8,128)} %measured_hbm.1, s32[16,8,32]{2,1,0:T(8,128)} %mask_hbm.1, f32[27,2,16,64]{3,2,1,0:T(8,128)} %kernel_hbm.1), custom_call_target="tpu_custom_call" | custom-call | tf_op jit(solution)/shard_map/pallas_call | solution.py:688
  41.5 1.7 %shard_map.38 = f32[2,16,16,8,32]{4,3,2,1,0:T(8,128)} custom-call(f32[4,8,2,16,128]{4,3,2,1,0:T(8,128)S(1)} %shard_map.37.packed), custom_call_target="tpu_custom_call" | custom-call | tf_op jit(solution)/shard_map/pallas_call | solution.py:721

commit v6 on v5

--- a/solution.py
+++ b/solution.py
@@ -93,11 +93,6 @@
         m = group_of(h, lax.rem(i, nc))
         return jnp.where(i < nc, groups - 1 - m, m)
 
-    load_mask.start()
-    load_kernel.start()
-    for i in range(groups):
-        load(step_group(i)).start()
-
     def home_same(cx):
         return {"kz": z, "coil": cx, "kx": kxh}
 
@@ -133,6 +128,11 @@
         def _():
             greet(near[d]["device"])
         count = count + near[d]["good"].astype(jnp.int32)
+
+    load_mask.start()
+    load_kernel.start()
+    for i in range(groups):
+        load(step_group(i)).start()
 
     def remote(src, dst, send, recv, device):
         return pltpu.make_async_remote_copy(
@@ -313,7 +313,8 @@
         kernel_last(d).wait_recv()
         weights(lax.rem(c + d, nc))
 
-    turn = reversal(lanes)
+    turns = {n: reversal(n) for n in sorted({lanes, plane, planes * row, row})}
+    turn = turns[lanes]
     eye = (lax.broadcasted_iota(jnp.int32, (lanes, lanes), 0) == lax.broadcasted_iota(jnp.int32, (lanes, lanes), 1))
     both = jnp.concatenate([jnp.where(eye, 1.0, 0.0).astype(BF16), turn], 1)
     def put(step, x, k, n, at):
@@ -400,7 +401,7 @@
 
     def flipped(x, rows):
         hi, lo = split(x)
-        y = jnp.dot(reversal(rows), jnp.concatenate([hi, lo], 1), preferred_element_type=F32)
+        y = jnp.dot(turns[rows], jnp.concatenate([hi, lo], 1), preferred_element_type=F32)
         return swap(y[:, :chans] + y[:, chans:])
 
     def place_halo(step, flip, buf, k, n, at):
@@ -602,21 +603,14 @@
         merge(jnp.where(i < nc, m, groups - 1 - m))
         return 0
 
-    lax.fori_loop(0, groups, home, 0)
-
     def sent(n, _):
         for q in range(halves):
             for i in range(nc):
                 far_copy(i, n, q).wait_send()
-                far_back(i, n, q).wait_send()
 
                 @pl.when(jnp.logical_not(is_self(i)))
                 def _():
                     same_copy(i, n, q).wait_send()
-
-                @pl.when(jnp.logical_not(stays & (c == i)))
-                def _():
-                    same_back(i, n, q).wait_send()
 
         return 0
 
@@ -645,6 +639,26 @@
         return 0
 
     lax.fori_loop(0, ITERS, passed, 0)
+
+    def returned(n, _):
+        for q in range(halves):
+            for i in range(nc):
+                far_back(i, n, q).wait_send()
+
+                @pl.when(jnp.logical_not(stays & (c == i)))
+                def _():
+                    same_back(i, n, q).wait_send()
+
+        return 0
+
+    def gather(i, _):
+        @pl.when(i == nc)
+        def _():
+            lax.fori_loop(0, parts, returned, 0)
+
+        return home(i, 0)
+
+    lax.fori_loop(0, groups, gather, 0)
 
 
 def unpack(packed, out_hbm, out, sem):

time: 43.8 us -> 43.7 us (level)
  no operation moved by 1% of the time
where the time goes in v6:
time: 43.7 us; the launch traced here: 43 us
  Pallas kernels  43 us (98%)
    pallas_call x1, Pallas kernels, on_device(): pl.pallas_call(functools.partial(body, sizes), out_shape=jax.ShapeDtypeSt...  41.3 us
    pallas_call x1, Pallas kernels, on_device(): pl.pallas_call(unpack, out_shape=jax.ShapeDtypeStruct(measured.shape, F32...  1.74 us

profile of v6, /device:TPU:9, one launch (start us, length us, event | category | flops | bytes accessed | tf_op | source)
XLA Modules:
  0.0 43.0 jit_solution(1340160862122186959)
XLA Ops:
  0.0 41.3 %shard_map.37.packed = f32[4,8,2,16,128]{4,3,2,1,0:T(8,128)S(1)} custom-call(f32[2,16,16,8,32]{4,3,2,1,0:T(8,128)} %measured_hbm.1, s32[16,8,32]{2,1,0:T(8,128)} %mask_hbm.1, f32[27,2,16,64]{3,2,1,0:T(8,128)} %kernel_hbm.1), custom_call_target="tpu_custom_call" | custom-call | tf_op jit(solution)/shard_map/pallas_call | solution.py:702
  41.3 1.7 %shard_map.38 = f32[2,16,16,8,32]{4,3,2,1,0:T(8,128)} custom-call(f32[4,8,2,16,128]{4,3,2,1,0:T(8,128)S(1)} %shard_map.37.packed), custom_call_target="tpu_custom_call" | custom-call | tf_op jit(solution)/shard_map/pallas_call | solution.py:735

commit v7 on v6

--- a/solution.py
+++ b/solution.py
@@ -533,10 +533,10 @@
         r = jnp.stack([x[:, i] for i in pair(q)], 1).reshape(lanes, chans)
         back = jnp.dot(turn2, jnp.concatenate(split(r), 0), preferred_element_type=F32)
         y = jnp.where(first, r, back).T.reshape(2, 2, nc, coils, lanes)
-        ob[slot(n, q), :, 0] = y[:, 0]
         ob[back_slot(n, q), :, 1] = y[:, 1]
         for cx in range(nc):
             far_back(cx, n, q).start()
+        ob[slot(n, q), :, 0] = y[:, 0]
         for cx in range(nc):
             @pl.when(jnp.logical_not(stays & (c == cx)))
             def _():

time: 43.7 us -> 43.6 us (level)
  no operation moved by 1% of the time
where the time goes in v7:
time: 43.6 us; the launch traced here: 43 us
  Pallas kernels  43 us (99%)
    pallas_call x1, Pallas kernels, on_device(): pl.pallas_call(functools.partial(body, sizes), out_shape=jax.ShapeDtypeSt...  41.2 us
    pallas_call x1, Pallas kernels, on_device(): pl.pallas_call(unpack, out_shape=jax.ShapeDtypeStruct(measured.shape, F32...  1.74 us

profile of v7, /device:TPU:9, one launch (start us, length us, event | category | flops | bytes accessed | tf_op | source)
XLA Modules:
  0.0 43.0 jit_solution(15921372455578624408)
XLA Ops:
  0.0 41.2 %shard_map.37.packed = f32[4,8,2,16,128]{4,3,2,1,0:T(8,128)S(1)} custom-call(f32[2,16,16,8,32]{4,3,2,1,0:T(8,128)} %measured_hbm.1, s32[16,8,32]{2,1,0:T(8,128)} %mask_hbm.1, f32[27,2,16,64]{3,2,1,0:T(8,128)} %kernel_hbm.1), custom_call_target="tpu_custom_call" | custom-call | tf_op jit(solution)/shard_map/pallas_call | solution.py:702
  41.3 1.7 %shard_map.38 = f32[2,16,16,8,32]{4,3,2,1,0:T(8,128)} custom-call(f32[4,8,2,16,128]{4,3,2,1,0:T(8,128)S(1)} %shard_map.37.packed), custom_call_target="tpu_custom_call" | custom-call | tf_op jit(solution)/shard_map/pallas_call | solution.py:735
